TPU v7x, 512 devices: a whole 4x8x8 slice. The times are simulated.
512 devices in a mesh: az: 32 (over z, x), ax: 16 (over y, core).
Axes of the slice: x: 4, y: 8, z: 8, core: 2. Of those that a mesh axis runs over, the one named last changes fastest.
Arguments:
- state: float32 [24576, 5, 512], P(('az', 'ax')), may hold values from -6 to 6
- velocity: float32 [24576, 3], P(('az', 'ax')), may hold values from -4 to 4
- interp_maps: float32 [24576, 3, 8, 8], P(('az', 'ax')), may hold values from -2 to 2
- neighbours: int32 [24576, 6], P(('az', 'ax')), may hold values from 0 to 1055
- send_faces: int32 [24576], P(('az', 'ax')), may hold values from 0 to 287
- owner_device: int32 [24576, 1], P(('az', 'ax')), may hold values from 0 to 31; in each aligned block of 48 rows (0 to 47, 48 to 95, ...) at most 3 rows name the same one
- owner_block: int32 [24576], P(('az', 'ax')), may hold values from 0 to 7
Outputs:
- new_state: float32 [24576, 5, 512], P(('az', 'ax'))
- spectrum: float32 [2, 5, 4096, 512], P(None, None, ('az', 'ax'))
Inputs may be any that keep to these rules, and one draw needn't show every extreme that they name: `owner_device`: in the rows of one device at most 3 elements name the same owner sector, and 3 is reached in some device.
All inputs are finite; a program needn't handle non-finite values.
Results may differ from a plain program's by a relative error of at most 0.0003.
Values sent between devices are 32-bit elements; how exact they have to be, the bound alone decides.
A program may use at most 64 MiB of HBM per device.

v0:
```python
import functools

import jax
import jax.numpy as jnp
import ml_dtypes
import numpy as np
from jax import lax
from jax.experimental import pallas as pl
from jax.experimental.pallas import tpu as pltpu
from jax.sharding import PartitionSpec as P

MESH = pl.DeviceIdType.MESH
F32 = jnp.float32
BF16 = jnp.bfloat16
E = 48
C = 5
ROWS = 6 * E
HALF = E // 2
STEP = 0.02
LIFT = 0.02 * 5.0


def spectral_derivative():
    points = np.cos(np.pi * np.arange(8) / 7.0)
    ends = (np.arange(8) == 0) | (np.arange(8) == 7)
    scales = np.where(ends, 2.0, 1.0)
    signs = np.where(np.arange(8) % 2 == 0, 1.0, -1.0)
    differ = points[:, None] - points[None, :]
    offdiag = (
        scales[:, None]
        / scales[None, :]
        * signs[:, None]
        * signs[None, :]
        / np.where(np.eye(8) > 0, 1.0, differ)
    )
    inner = -points / (2.0 * np.where(ends, 1.0, 1.0 - points * points))
    corner = (2.0 * 49.0 + 1.0) / 6.0
    diagonal = np.where(np.arange(8) == 0, corner, np.where(np.arange(8) == 7, -corner, inner))
    return np.where(np.eye(8) > 0, diagonal[:, None], offdiag)


DERIV = [[float(np.float32(v)) for v in row] for row in spectral_derivative()]


def dft_tables():
    tp, t2, j = np.meshgrid(np.arange(4), np.arange(2), np.arange(64), indexing="ij")
    theta = (8 * j + 2 * tp + t2).reshape(-1)
    phase = (theta[:, None] * np.arange(512)[None, :]) % 512
    angle = phase * (2.0 * np.pi / 512)
    table = np.concatenate([np.cos(angle), -np.sin(angle)], axis=1) * 512**-0.5
    high = table.astype(ml_dtypes.bfloat16)
    low = (table - high.astype(np.float64)).astype(ml_dtypes.bfloat16)
    return np.stack([high, low])


TABLES = dft_tables()


def contract(coef, tiles):
    total = coef(0) * tiles[0]
    for k in range(1, len(tiles)):
        total = total + coef(k) * tiles[k]
    return total


def kernel(
    n_ax,
    state_ref,
    vel_ref,
    maps_ref,
    owner_ref,
    block_ref,
    nbr_ref,
    send_ref,
    dft_ref,
    new_ref,
    spec_ref,
    flat,
    u,
    a,
    b,
    b2,
    vel,
    mt,
    fr,
    local,
    tab0,
    tab1,
    gat,
    wt,
    xs,
    xr,
    acc,
    zs,
    zr,
    dft,
    ag_send,
    up_recv,
    dn_recv,
    sib_recv,
    x_send,
    x_recv,
    z_send,
    z_recv,
    dft_sem,
):
    az, ax = lax.axis_index("az"), lax.axis_index("ax")
    z, x = az // 4, az % 4
    up, dn = lax.rem(ax + 2, n_ax), lax.rem(ax + n_ax - 2, n_ax)
    sib = ax + 1 - 2 * lax.rem(ax, 2)

    tabs = (tab0, tab1)
    barrier = pltpu.get_barrier_semaphore()
    for peer in (up, dn, sib):
        pl.semaphore_signal(barrier, inc=1, device_id=(az, peer), device_id_type=MESH)
    for d in range(1, 4):
        pl.semaphore_signal(
            barrier, inc=1, device_id=(z * 4 + lax.rem(x + d, 4), ax), device_id_type=MESH
        )
    for d in range(1, 8):
        pl.semaphore_signal(
            barrier, inc=1, device_id=(lax.rem(z + d, 8) * 4 + x, ax), device_id_type=MESH
        )

    dft_copy = pltpu.make_async_copy(dft_ref, dft, dft_sem)
    dft_copy.start()

    lane = lax.broadcasted_iota(jnp.int32, (8, 128), 1)

    def low_half(rows):
        return lax.broadcasted_iota(jnp.int32, (rows, 128), 1) < 64

    flat[0:240] = state_ref[...]
    flat[240:256] = jnp.zeros((16, 512), F32)
    for h in range(2):
        for n in range(4):
            u[h, 128 * n : 128 * n + 128, :] = flat[
                128 * h : 128 * h + 128, 128 * n : 128 * n + 128
            ].T

    def face_pair(ref, h, pair):
        if pair == 0:
            return jnp.concatenate([ref[h, 0:64, :], ref[h, 448:512, :]], axis=0)
        if pair == 1:
            return jnp.concatenate(
                [ref[h, 64 * i + o : 64 * i + o + 8, :] for o in (0, 56) for i in range(8)], axis=0
            )
        return jnp.concatenate(
            [ref[h, pl.ds(0, 64, stride=8), :], ref[h, pl.ds(7, 64, stride=8), :]], axis=0
        )

    def publish(ref, g):
        for pair in range(3):
            for h in range(2):
                fr[pair, 128 * h : 128 * h + 128, :] = face_pair(ref, h, pair).T
        for pair in range(3):
            for p in range(3):
                first = fr[pair, 96 * p : 96 * p + 48, :]
                if p < 2:
                    second = fr[pair, 96 * p + 48 : 96 * p + 96, :]
                else:
                    second = jnp.zeros((48, 128), F32)
                low = low_half(48)
                even = jnp.where(low, first, pltpu.roll(second, 64, 1))
                odd = jnp.where(low, pltpu.roll(first, 64, 1), second)
                for table in (local, tabs[g]):
                    table[p, pl.ds(2 * pair, 48, stride=6), :] = even
                    table[p, pl.ds(2 * pair + 1, 48, stride=6), :] = odd
        own = pl.multiple_of(ROWS + E * ax, 8)

        @pl.loop(0, 12)
        def _(i):
            for k in range(4):
                s = 4 * i + k
                tabs[g][:, pl.ds(own + s, 1), :] = local[:, pl.ds(send_ref[0, s], 1), :]

    def ag_copy(g, source, ch, target, send, recv):
        rows = pl.ds(pl.multiple_of(ROWS + E * source + HALF * ch, 8), HALF)
        return pltpu.make_async_remote_copy(
            src_ref=tabs[g].at[:, rows, :],
            dst_ref=tabs[g].at[:, rows, :],
            send_sem=send,
            recv_sem=recv,
            device_id=(az, target),
            device_id_type=MESH,
        )

    def below(base, h):
        return lax.rem(base + n_ax - 2 * h, n_ax)

    def above(base, h):
        return lax.rem(base + 2 * h, n_ax)

    arrivals = [
        (h, ch, rising)
        for h in range(1, 5)
        for ch in range(2)
        for rising in (True, False)
        if h < 4 or (ch == 0) == rising
    ]

    class Gather:
        def __init__(self, g):
            self.g = g
            self.sent = []

        def send(self, source, ch, target, recv):
            copy = ag_copy(self.g, source, ch, target, ag_send.at[self.g, len(self.sent)], recv)
            copy.start()
            self.sent.append(copy)

        def start(self):
            g = self.g
            for ch in range(2):
                self.send(ax, ch, up, up_recv.at[g, 0, ch])
                self.send(ax, ch, dn, dn_recv.at[g, 0, ch])
            for ch in range(2):
                self.send(ax, ch, sib, sib_recv.at[g, ch])

        def hop(self, hops):
            g = self.g
            for k, (h, ch, rising) in enumerate(arrivals):
                if h != hops:
                    continue
                source = below(ax, h) if rising else above(ax, h)
                sems = up_recv if rising else dn_recv
                target = up if rising else dn
                ag_copy(
                    g, source, ch, target, ag_send.at[g, 0], sems.at[g, h - 1, ch]
                ).wait_recv()
                if h < 3 or (h == 3 and (ch == 0) == rising):
                    self.send(source, ch, target, sems.at[g, h, ch])
                self.send(source, ch, sib, sib_recv.at[g, 2 + k])

        def finish(self):
            g = self.g
            for ch in range(2):
                ag_copy(g, sib, ch, sib, ag_send.at[g, 0], sib_recv.at[g, ch]).wait_recv()
            for k, (h, ch, rising) in enumerate(arrivals):
                source = below(sib, h) if rising else above(sib, h)
                ag_copy(g, source, ch, sib, ag_send.at[g, 0], sib_recv.at[g, 2 + k]).wait_recv()

        def drain(self):
            for copy in self.sent:
                copy.wait_send()

    def along_x(src, dst):
        @pl.loop(0, 8)
        def _(y):
            for h in range(2):
                rows = [pl.ds(pl.multiple_of(64 * i + 8 * y, 8), 8) for i in range(8)]
                tiles = [src[h, rows[i], :] for i in range(8)]
                v = vel[0, h]
                for i in range(8):
                    dst[h, rows[i], :] = tiles[i] + v * contract(lambda k: DERIV[i][k], tiles)

    def along_yz(src, dst):
        @pl.loop(0, 8)
        def _(i):
            for h in range(2):
                rows = [pl.ds(pl.multiple_of(64 * i + 8 * y, 8), 8) for y in range(8)]
                tiles = [src[h, rows[y], :] for y in range(8)]
                v = vel[1, h]
                for y in range(8):
                    dst[h, rows[y], :] += v * contract(lambda k: DERIV[y][k], tiles)
                cols = [pl.ds(64 * i + q, 8, stride=8) for q in range(8)]
                tiles = [src[h, cols[q], :] for q in range(8)]
                v = vel[2, h]
                for q in range(8):
                    dst[h, cols[q], :] += v * contract(lambda k: DERIV[q][k], tiles)

    def lift(dst, value, scale):
        for h in range(2):
            dst[h, 0:64, :] += scale * value(h, 0)
            dst[h, 448:512, :] += scale * value(h, 1)
            for f, o in ((2, 0), (3, 56)):
                rows = scale * value(h, f)
                for i in range(8):
                    dst[h, 64 * i + o : 64 * i + o + 8, :] += rows[8 * i : 8 * i + 8]
            dst[h, pl.ds(0, 64, stride=8), :] += scale * value(h, 4)
            dst[h, pl.ds(7, 64, stride=8), :] += scale * value(h, 5)

    def own_face(ref):
        def value(h, f):
            pair = face_pair(ref, h, f // 2)
            return pair[64 * (f % 2) : 64 * (f % 2) + 64]

        return value

    def facing(g):
        @pl.loop(0, E)
        def _(e):
            for f in range(6):
                gat[:, pl.ds(f * E + e, 1), :] = tabs[g][:, pl.ds(nbr_ref[f, e], 1), :]

        for pair in range(3):
            for c in range(C):
                first = gat[c // 2, 96 * pair : 96 * pair + 48, :]
                second = gat[c // 2, 96 * pair + 48 : 96 * pair + 96, :]
                low = low_half(48)
                if c % 2 == 0:
                    both = jnp.where(low, first, pltpu.roll(second, 64, 1))
                else:
                    both = jnp.where(low, pltpu.roll(first, 64, 1), second)
                fr[pair, 48 * c : 48 * c + 48, :] = both
            for h in range(2):
                wt[h, 128 * pair : 128 * pair + 128, :] = fr[
                    pair, 128 * h : 128 * h + 128, :
                ].T

    def from_wt(h, f):
        return wt[h, 64 * f : 64 * f + 64, :]

    publish(u, 0)
    pl.semaphore_wait(barrier, 13)
    gather = Gather(0)
    gather.start()

    spread = (
        lax.rem(lax.broadcasted_iota(jnp.int32, (E, 256), 1), E)
        == lax.broadcasted_iota(jnp.int32, (E, 256), 0)
    ) & (lax.broadcasted_iota(jnp.int32, (E, 256), 1) < C * E)
    spread = spread.astype(F32)

    def over_lanes(rows):
        return jnp.dot(rows, spread, precision=lax.Precision.HIGHEST, preferred_element_type=F32)

    speeds = over_lanes(-STEP * vel_ref[...])
    maps = over_lanes(maps_ref[...])
    block = block_ref[...]
    label = lax.rem(block, 4) * 64 + owner_ref[...] * 2 + block // 4
    labels = over_lanes(label.astype(F32))
    for h in range(2):
        for d in range(3):
            vel[d, h] = jnp.broadcast_to(speeds[d : d + 1, 128 * h : 128 * h + 128], (8, 128))
        mt[h] = maps[:, 128 * h : 128 * h + 128]
        for d in range(4):
            xs[d, h, 128:136, :] = jnp.broadcast_to(
                labels[:, 128 * h : 128 * h + 128], (8, 128)
            )

    fr[:, 240:256, :] = jnp.zeros((3, 16, 128), F32)
    along_x(u, a)
    gather.hop(1)
    along_yz(u, a)
    gather.hop(2)
    lift(a, own_face(u), -LIFT)
    gather.hop(3)
    gather.hop(4)
    gather.finish()
    facing(0)
    lift(a, from_wt, LIFT)

    publish(a, 1)
    gather2 = Gather(1)
    gather2.start()
    along_x(a, b)
    gather2.hop(1)
    along_yz(a, b)
    gather2.hop(2)
    lift(b, own_face(a), -LIFT)
    b[...] = 0.5 * (u[...] + b[...])
    gather2.hop(3)
    gather2.hop(4)
    gather2.finish()
    facing(1)
    lift(b, from_wt, 0.5 * LIFT)

    def coef(h, which, out):
        return lambda k: mt[h, pl.ds(64 * which + 8 * out + k, 1), :]

    @pl.loop(0, 8)
    def _(y):
        for h in range(2):
            rows = [pl.ds(pl.multiple_of(64 * i + 8 * y, 8), 8) for i in range(8)]
            tiles = [b[h, rows[i], :] for i in range(8)]
            for r in range(8):
                b2[h, rows[r], :] = contract(coef(h, 1, r), tiles)

    @pl.loop(0, 8)
    def _(r):
        for h in range(2):
            rows = [pl.ds(pl.multiple_of(64 * r + 8 * i, 8), 8) for i in range(8)]
            tiles = [b2[h, rows[i], :] for i in range(8)]
            for t in range(8):
                a[h, rows[t], :] = contract(coef(h, 0, t), tiles)
            tiles = [a[h, pl.ds(64 * r + q, 8, stride=8), :] for q in range(8)]
            for q in range(8):
                xs[r % 4, h, pl.ds((r // 4) * 64 + q, 8, stride=8), :] = contract(
                    coef(h, 2, q), tiles
                )

    x_copies = []
    for d in (1, 3, 2):
        target = lax.rem(x + d, 4)
        copy = pltpu.make_async_remote_copy(
            src_ref=xs.at[target],
            dst_ref=xr.at[d - 1],
            send_sem=x_send.at[d - 1],
            recv_sem=x_recv.at[d - 1],
            device_id=(z * 4 + target, ax),
            device_id_type=MESH,
        )
        copy.start()
        x_copies.append(copy)

    for h in range(2):
        for n in range(4):
            flat[128 * h : 128 * h + 128, 128 * n : 128 * n + 128] = b[
                h, 128 * n : 128 * n + 128, :
            ].T
    new_ref[...] = flat[0:240]

    wide = lax.broadcasted_iota(jnp.int32, (128, 256), 1)

    def collect(ref, first):
        values = jnp.concatenate([ref[0, 0:128, :], ref[1, 0:128, :]], axis=1)
        names = jnp.concatenate([ref[0, 128:129, :], ref[1, 128:129, :]], axis=1)
        place = (
            lax.broadcasted_iota(jnp.int32, (256, 256), 0) == names.astype(jnp.int32)
        ).astype(BF16)
        high = values.astype(BF16).astype(F32)
        low = values - high
        for c in range(C):
            mine = (wide >= E * c) & (wide < E * c + E)
            part = 0.0
            for term in (high, low):
                part = part + lax.dot_general(
                    jnp.where(mine, term, 0.0).astype(BF16),
                    place,
                    (((1,), (1,)), ((), ())),
                    preferred_element_type=F32,
                )
            if first:
                acc[c] = part
            else:
                acc[c] += part

    collect(xs.at[x], True)
    for copy, d in zip(x_copies, (1, 3, 2)):
        copy.wait_recv()
        collect(xr.at[d - 1], False)

    low8 = lane < 64
    for c in range(C):
        for r2 in range(2):
            for tp in range(4):
                o = 64 * r2 + 16 * tp
                for v in range(2):
                    even = acc[c, o : o + 8, 128 * v : 128 * v + 128]
                    odd = acc[c, o + 8 : o + 16, 128 * v : 128 * v + 128]
                    zs[4 * v + r2, c, tp] = jnp.where(low8, even, pltpu.roll(odd, 64, 1))
                    zs[4 * v + 2 + r2, c, tp] = jnp.where(low8, pltpu.roll(even, 64, 1), odd)

    z_copies = []
    for d in (4, 3, 5, 2, 6, 1, 7):
        target = lax.rem(z + d, 8)
        copy = pltpu.make_async_remote_copy(
            src_ref=zs.at[target],
            dst_ref=zr.at[d - 1],
            send_sem=z_send.at[d - 1],
            recv_sem=z_recv.at[d - 1],
            device_id=(target * 4 + x, ax),
            device_id_type=MESH,
        )
        copy.start()
        z_copies.append(copy)

    total = zs[z]
    for copy, d in reversed(list(zip(z_copies, (4, 3, 5, 2, 6, 1, 7)))):
        copy.wait_recv()
        total = total + zr[d - 1]

    dft_copy.wait()
    series = jnp.concatenate([total[:, tp].reshape(8 * C, 128) for tp in range(4)], axis=1)
    high = series.astype(BF16)
    low = (series - high.astype(F32)).astype(BF16)
    for half in range(2):
        cols = pl.ds(512 * half, 512)
        spec_ref[half] = (
            jnp.dot(high, dft[0, :, cols], preferred_element_type=F32)
            + jnp.dot(low, dft[0, :, cols], preferred_element_type=F32)
            + jnp.dot(high, dft[1, :, cols], preferred_element_type=F32)
        )

    gather.drain()
    gather2.drain()
    for copy in x_copies + z_copies:
        copy.wait_send()


def per_device(n_ax, state, velocity, interp_maps, neighbours, send_faces, owner_device, owner_block):
    vmem = pl.BlockSpec(memory_space=pltpu.VMEM)
    smem = pl.BlockSpec(memory_space=pltpu.SMEM)
    dma = pltpu.SemaphoreType.DMA
    half_nodes = pltpu.VMEM((2, 512, 128), F32)
    new, spec = pl.pallas_call(
        functools.partial(kernel, n_ax),
        out_shape=(
            jax.ShapeDtypeStruct((C * E, 512), F32),
            jax.ShapeDtypeStruct((2, 8 * C, 512), F32),
        ),
        in_specs=[vmem] * 5 + [smem] * 2 + [pl.BlockSpec(memory_space=pl.ANY)],
        out_specs=(vmem, vmem),
        scratch_shapes=[
            pltpu.VMEM((256, 512), F32),
            half_nodes,
            half_nodes,
            half_nodes,
            half_nodes,
            pltpu.VMEM((3, 2, 8, 128), F32),
            pltpu.VMEM((2, 192, 128), F32),
            pltpu.VMEM((3, 256, 128), F32),
            pltpu.VMEM((3, ROWS, 128), F32),
            pltpu.VMEM((3, ROWS + E * n_ax, 128), F32),
            pltpu.VMEM((3, ROWS + E * n_ax, 128), F32),
            pltpu.VMEM((3, ROWS, 128), F32),
            pltpu.VMEM((2, 384, 128), F32),
            pltpu.VMEM((4, 2, 136, 128), F32),
            pltpu.VMEM((3, 2, 136, 128), F32),
            pltpu.VMEM((C, 128, 256), F32),
            pltpu.VMEM((8, C, 4, 8, 128), F32),
            pltpu.VMEM((7, C, 4, 8, 128), F32),
            pltpu.VMEM((2, 512, 1024), BF16),
            dma((2, 30)),
            dma((2, 4, 2)),
            dma((2, 4, 2)),
            dma((2, 16)),
            dma((3,)),
            dma((3,)),
            dma((7,)),
            dma((7,)),
            dma,
        ],
        compiler_params=pltpu.CompilerParams(
            collective_id=0, has_side_effects=True, vmem_limit_bytes=56 * 1024 * 1024
        ),
        name="advance",
    )(
        state.transpose(1, 0, 2).reshape(C * E, 512),
        velocity.T,
        interp_maps.transpose(1, 2, 3, 0).reshape(192, E),
        owner_device.reshape(1, E),
        owner_block.reshape(1, E),
        neighbours.T,
        send_faces.reshape(1, E),
        jnp.asarray(TABLES),
    )
    return (
        new.reshape(C, E, 512).transpose(1, 0, 2),
        spec.reshape(2, C, 8, 512),
    )


def solution(mesh):
    return jax.shard_map(
        functools.partial(per_device, mesh.shape["ax"]),
        mesh=mesh,
        in_specs=(
            P(("az", "ax"), None, None),
            P(("az", "ax"), None),
            P(("az", "ax"), None, None, None),
            P(("az", "ax"), None),
            P(("az", "ax")),
            P(("az", "ax"), None),
            P(("az", "ax")),
        ),
        out_specs=(P(("az", "ax"), None, None), P(None, None, ("az", "ax"), None)),
        check_vma=False,
    )
```

profile of v0, /device:TPU:8, one launch (start us, length us, event | category | flops | bytes accessed | tf_op | source)
XLA Modules:
  0.0 79.9 jit_solution(13016997138164629080)
XLA Ops:
  0.6 75.8 %advance.1 = (f32[240,512]{1,0:T(8,128)}, f32[2,40,512]{2,1,0:T(8,128)}) custom-call(f32[240,512]{1,0:T(8,128)} %bitcast.15, f32[3,48]{1,0:T(4,128)} %bitcast.20, f32[192,48]{1,0:T(8,128)} %bitcast.18, s32[1,48]{1,0:T(1,128)} %bitcast.21, s32[1,48]{1,0:T(1,128)} %bitcast.22, s32[6,48]{1,0:T(8,128)} %bitcast.19, s32[1,48]{1,0:T(1,128)} %bitcast.23, ...), custom_call_target="tpu_custom_call" | custom-call | tf_op jit(solution)/shard_map/advance/pallas_call | solution.py:497
  76.4 1.9 %copy.12 = f32[48,5,512]{2,0,1:T(8,128)} copy(f32[48,5,512]{2,0,1:T(8,128)} %bitcast.16) | data formatting | bytes 983040
  78.3 1.6 %copy.13 = f32[2,5,8,512]{3,2,1,0:T(8,128)} copy(f32[2,5,8,512]{3,2,1,0:T(8,128)} %bitcast.17) | data formatting | bytes 327680
where the time goes:
time: 80.2 us; the launch traced here: 79.9 us
  Pallas kernels  75.8 us (95%)
  local copies, waits for them, and re-layouts  3.45 us (4%)
    pallas_call x1, Pallas kernels, per_device(): pl.pallas_call(functools.partial(kernel, n_ax), out_shape=(jax.ShapeDtype...  75.8 us
    unnamed x2, local copies, waits for them, and re-layouts  3.45 us

commit v1 on v0

v1 whole, which is shorter than its diff:
```python
import functools

import jax
import jax.numpy as jnp
import ml_dtypes
import numpy as np
from jax import lax
from jax.experimental import pallas as pl
from jax.experimental.pallas import tpu as pltpu
from jax.sharding import PartitionSpec as P

MESH = pl.DeviceIdType.MESH
F32 = jnp.float32
BF16 = jnp.bfloat16
E = 48
C = 5
ROWS = 6 * E
CHAINED = ()
Z_STEPS = 5 * len(CHAINED) + 2 * (4 - len(CHAINED))
Z_ENDS = 2 * len(CHAINED) + 4 * (4 - len(CHAINED))
BLOCK = 120
PIECES = ((0, 64), (64, 56))
STEP = 0.02
LIFT = 0.02 * 5.0


def spectral_derivative():
    points = np.cos(np.pi * np.arange(8) / 7.0)
    ends = (np.arange(8) == 0) | (np.arange(8) == 7)
    scales = np.where(ends, 2.0, 1.0)
    signs = np.where(np.arange(8) % 2 == 0, 1.0, -1.0)
    differ = points[:, None] - points[None, :]
    offdiag = (
        scales[:, None]
        / scales[None, :]
        * signs[:, None]
        * signs[None, :]
        / np.where(np.eye(8) > 0, 1.0, differ)
    )
    inner = -points / (2.0 * np.where(ends, 1.0, 1.0 - points * points))
    corner = (2.0 * 49.0 + 1.0) / 6.0
    diagonal = np.where(np.arange(8) == 0, corner, np.where(np.arange(8) == 7, -corner, inner))
    return np.where(np.eye(8) > 0, diagonal[:, None], offdiag)


DERIV = [[float(np.float32(v)) for v in row] for row in spectral_derivative()]


def dft_tables():
    j, m0 = np.meshgrid(np.arange(64), np.arange(64), indexing="ij")
    angle = (j * m0 % 64) * (2.0 * np.pi / 64)
    points = np.concatenate([np.cos(angle)] * 2 + [-np.sin(angle)] * 2, axis=1)
    table = np.zeros((2, 64, 2, 256))
    table[0, :, 0], table[1, :, 1] = points, points
    table = table.reshape(128, 512)
    high = table.astype(ml_dtypes.bfloat16)
    low = (table - high.astype(np.float64)).astype(ml_dtypes.bfloat16)
    t, m = np.meshgrid(np.arange(8), np.arange(512), indexing="ij")
    angle = (t * m % 512) * (2.0 * np.pi / 512)
    twiddle = np.stack([np.cos(angle), -np.sin(angle)]) * 512**-0.5
    return np.stack([high, low]), twiddle.astype(np.float32)


TABLES, TWIDDLE = dft_tables()


def contract(coef, tiles):
    total = coef(0) * tiles[0]
    for k in range(1, len(tiles)):
        total = total + coef(k) * tiles[k]
    return total


def kernel(
    n_ax,
    vel_hbm,
    maps_hbm,
    owner_hbm,
    block_hbm,
    nbv_hbm,
    send_hbm,
    state_ref,
    new_ref,
    sum_hbm,
    sum_ref,
    flat,
    u,
    a,
    b,
    b2,
    vel,
    mt,
    fr,
    local,
    last,
    tab0,
    tab1,
    gat,
    where_v,
    where,
    upper,
    vel_ref,
    maps_ref,
    owner_ref,
    block_ref,
    nbv_ref,
    send_ref,
    in_sem,
    where_sem,
    wt,
    names,
    names_in,
    place,
    xs,
    xr,
    zs,
    zr,
    state_sem,
    new_sem,
    ag_send,
    y_recv,
    sib_recv,
    name_send,
    name_recv,
    x_send,
    x_recv,
    z_send,
    z_recv,
    z_last,
):
    az, ax = lax.axis_index("az"), lax.axis_index("ax")
    z, x = az // 4, az % 4
    up, dn = lax.rem(ax + 2, n_ax), lax.rem(ax + n_ax - 2, n_ax)
    up2, dn2 = lax.rem(ax + 4, n_ax), lax.rem(ax + n_ax - 4, n_ax)
    sib = ax + 1 - 2 * lax.rem(ax, 2)
    far = BLOCK * n_ax

    tabs = (tab0, tab1)
    state_copies = [
        pltpu.make_async_copy(state_ref.at[:, part], flat.at[0:240, part], state_sem.at[n])
        for n, part in enumerate((pl.ds(0, 256), pl.ds(256, 256)))
    ]
    operand_copies = [
        pltpu.make_async_copy(src, dst, in_sem.at[n])
        for n, (src, dst) in enumerate(
            (
                (send_hbm, send_ref),
                (vel_hbm, vel_ref),
                (owner_hbm, owner_ref),
                (block_hbm, block_ref),
                (nbv_hbm, nbv_ref),
                (maps_hbm, maps_ref),
            )
        )
    ]
    for copy in state_copies + operand_copies:
        copy.start()
    barrier = pltpu.get_barrier_semaphore()
    for peer in (up, dn, up2, dn2, sib):
        pl.semaphore_signal(barrier, inc=1, device_id=(az, peer), device_id_type=MESH)
    for d in range(1, 4):
        pl.semaphore_signal(
            barrier, inc=1, device_id=(z * 4 + lax.rem(x + d, 4), ax), device_id_type=MESH
        )
    for d in (1, 2, 6, 7):
        pl.semaphore_signal(
            barrier, inc=1, device_id=(lax.rem(z + d, 8) * 4 + x, ax), device_id_type=MESH
        )

    lane = lax.broadcasted_iota(jnp.int32, (8, 128), 1)

    def low_half(rows):
        return lax.broadcasted_iota(jnp.int32, (rows, 128), 1) < 64

    flat[240:256] = jnp.zeros((16, 512), F32)
    for n in range(4):
        if n % 2 == 0:
            state_copies[n // 2].wait()
        for h in range(2):
            u[h, 128 * n : 128 * n + 128, :] = flat[
                128 * h : 128 * h + 128, 128 * n : 128 * n + 128
            ].T
    for copy in operand_copies:
        copy.wait()

    def face_pair(ref, h, pair):
        if pair == 0:
            return jnp.concatenate([ref[h, 0:64, :], ref[h, 448:512, :]], axis=0)
        if pair == 1:
            return jnp.concatenate(
                [ref[h, 64 * i + o : 64 * i + o + 8, :] for o in (0, 56) for i in range(8)], axis=0
            )
        return jnp.concatenate(
            [ref[h, pl.ds(0, 64, stride=8), :], ref[h, pl.ds(7, 64, stride=8), :]], axis=0
        )

    def publish(ref, g):
        for pair in range(3):
            for h in range(2):
                fr[pair, 128 * h : 128 * h + 128, :] = face_pair(ref, h, pair).T
        for pair in range(3):
            for p in range(3):
                first = fr[pair, 96 * p : 96 * p + 48, :]
                if p < 2:
                    second = fr[pair, 96 * p + 48 : 96 * p + 96, :]
                else:
                    second = jnp.zeros((48, 128), F32)
                low = low_half(48)
                even = jnp.where(low, first, pltpu.roll(second, 64, 1))
                odd = jnp.where(low, pltpu.roll(first, 64, 1), second)
                table = tabs[g]
                for o, rows in ((0, even), (1, odd)):
                    f = 2 * pair + o
                    local[p, pl.ds(f, 48, stride=6), :] = rows
                    if p < 2:
                        for k in range(6):
                            table[pl.ds(far + 96 * k + 48 * p + f, 8, stride=6), :] = rows[
                                8 * k : 8 * k + 8
                            ]
                    else:
                        table[pl.ds(far + 2 * ROWS + f, 48, stride=6), :] = rows
        own = pl.multiple_of(BLOCK * ax, 8)
        table = tabs[g]

        @pl.loop(0, 12)
        def _(i):
            for k in range(4):
                s = 4 * i + k
                row = send_ref[0, s]
                for p in range(2):
                    table[pl.ds(own + 48 * p + s, 1), :] = local[p, pl.ds(row, 1), :]
                last[pl.ds(s, 1), :] = local[2, pl.ds(row, 1), :]

        table[pl.ds(own + 96, 24), :] = jnp.where(
            low_half(24), last[0:24, :], pltpu.roll(last[24:48, :], 64, 1)
        )

    def ag_copy(g, source, piece, target, send, recv):
        start, count = PIECES[piece]
        rows = pl.ds(pl.multiple_of(BLOCK * source + start, 8), count)
        return pltpu.make_async_remote_copy(
            src_ref=tabs[g].at[rows, :],
            dst_ref=tabs[g].at[rows, :],
            send_sem=send,
            recv_sem=recv,
            device_id=(az, target),
            device_id_type=MESH,
        )

    def behind(way, h):
        return lax.rem(ax + (n_ax - 2 * h if way == 0 else 2 * h), n_ax)

    class Gather:
        ways = ((0, up, up2), (1, dn, dn2))

        def __init__(self, g):
            self.g = g
            self.sent = 0

        def send(self, source, piece, target, recv):
            ag_copy(self.g, source, piece, target, ag_send.at[self.g], recv).start()
            self.sent += PIECES[piece][1]

        def share(self, source, piece):
            self.send(source, piece, sib, sib_recv.at[self.g])

        def start(self):
            g = self.g
            for h in (1, 0):
                for k in range(2):
                    for way, *targets in self.ways:
                        piece = 1 - k if way else k
                        self.send(ax, piece, targets[h], y_recv.at[g, way, h, piece])
            for piece in range(2):
                self.share(ax, piece)

        def hop(self, h):
            g = self.g
            for k in range(2 if h < 4 else 1):
                for way, one, two in self.ways:
                    piece = 1 - k if way else k
                    source = behind(way, h)
                    ag_copy(
                        g, source, piece, one, ag_send.at[g], y_recv.at[g, way, h - 1, piece]
                    ).wait_recv()
                    if h == 2:
                        if k == 0:
                            self.send(source, piece, two, y_recv.at[g, way, 3, piece])
                        self.send(source, piece, one, y_recv.at[g, way, 2, piece])
                    self.share(source, piece)

        def whole(self, count):
            rows = pl.ds(0, count)
            return pltpu.make_async_remote_copy(
                src_ref=tabs[self.g].at[rows, :],
                dst_ref=tabs[self.g].at[rows, :],
                send_sem=ag_send.at[self.g],
                recv_sem=sib_recv.at[self.g],
                device_id=(az, sib),
                device_id_type=MESH,
            )

        def finish(self):
            self.whole(8 * BLOCK).wait_recv()

        def drain(self):
            self.whole(self.sent).wait_send()

    def along_x(src, dst):
        @pl.loop(0, 8)
        def _(y):
            for h in range(2):
                rows = [pl.ds(pl.multiple_of(64 * i + 8 * y, 8), 8) for i in range(8)]
                tiles = [src[h, rows[i], :] for i in range(8)]
                v = vel[0, h]
                for i in range(8):
                    dst[h, rows[i], :] = tiles[i] + v * contract(lambda k: DERIV[i][k], tiles)

    def along_yz(src, dst):
        @pl.loop(0, 8)
        def _(i):
            for h in range(2):
                rows = [pl.ds(pl.multiple_of(64 * i + 8 * y, 8), 8) for y in range(8)]
                tiles = [src[h, rows[y], :] for y in range(8)]
                v = vel[1, h]
                for y in range(8):
                    dst[h, rows[y], :] += v * contract(lambda k: DERIV[y][k], tiles)
                cols = [pl.ds(64 * i + q, 8, stride=8) for q in range(8)]
                tiles = [src[h, cols[q], :] for q in range(8)]
                v = vel[2, h]
                for q in range(8):
                    dst[h, cols[q], :] += v * contract(lambda k: DERIV[q][k], tiles)

    def lift(dst, value, scale):
        for h in range(2):
            dst[h, 0:64, :] += scale * value(h, 0)
            dst[h, 448:512, :] += scale * value(h, 1)
            for f, o in ((2, 0), (3, 56)):
                rows = scale * value(h, f)
                for i in range(8):
                    dst[h, 64 * i + o : 64 * i + o + 8, :] += rows[8 * i : 8 * i + 8]
            dst[h, pl.ds(0, 64, stride=8), :] += scale * value(h, 4)
            dst[h, pl.ds(7, 64, stride=8), :] += scale * value(h, 5)

    def own_face(ref):
        def value(h, f):
            pair = face_pair(ref, h, f // 2)
            return pair[64 * (f % 2) : 64 * (f % 2) + 64]

        return value

    def facing(g):
        size = far + 3 * ROWS - 48
        views = (tabs[g].at[pl.ds(0, size), :], tabs[g].at[pl.ds(48, size), :], tabs[g])

        @pl.loop(0, E)
        def _(e):
            for f in range(6):
                pair, single = where[f, e], where[8 + f, e]
                for p, row in enumerate((pair, pair, single)):
                    gat[p, pl.ds(f * E + e, 1), :] = views[p][pl.ds(row, 1), :]


        def got(p, f):
            rows = gat[p, f * E : f * E + E, :]
            if p < 2:
                return rows
            return jnp.where(upper[f * E : f * E + E, :] > 0.5, pltpu.roll(rows, 64, 1), rows)

        low = low_half(48)
        for pair in range(3):
            for p in range(3):
                first, second = got(p, 2 * pair), got(p, 2 * pair + 1)
                fr[pair, 96 * p : 96 * p + 48, :] = jnp.where(
                    low, first, pltpu.roll(second, 64, 1)
                )
                if p < 2:
                    fr[pair, 96 * p + 48 : 96 * p + 96, :] = jnp.where(
                        low, pltpu.roll(first, 64, 1), second
                    )
            for h in range(2):
                wt[h, 128 * pair : 128 * pair + 128, :] = fr[
                    pair, 128 * h : 128 * h + 128, :
                ].T

    def from_wt(h, f):
        return wt[h, 64 * f : 64 * f + 64, :]

    def moved(ref, send, recv):
        return pltpu.make_async_remote_copy(
            src_ref=ref,
            dst_ref=ref,
            send_sem=send,
            recv_sem=recv,
            device_id=(az, sib),
            device_id_type=MESH,
        )

    publish(u, 0)
    pl.semaphore_wait(barrier, 12)
    gather = Gather(0)
    gather.start()

    spread = (
        lax.rem(lax.broadcasted_iota(jnp.int32, (E, 256), 1), E)
        == lax.broadcasted_iota(jnp.int32, (E, 256), 0)
    ) & (lax.broadcasted_iota(jnp.int32, (E, 256), 1) < C * E)
    spread = spread.astype(F32)

    def over_lanes(rows):
        return jnp.dot(rows, spread, precision=lax.Precision.HIGHEST, preferred_element_type=F32)

    speeds = over_lanes(-STEP * vel_ref[...])
    block = block_ref[...]
    label = lax.rem(block, 4) * 64 + owner_ref[...] * 2 + block // 4
    labels = over_lanes(label.astype(F32))
    for h in range(2):
        names[h] = jnp.broadcast_to(labels[:, 128 * h : 128 * h + 128], (8, 128))
        for d in range(3):
            vel[d, h] = jnp.broadcast_to(speeds[d : d + 1, 128 * h : 128 * h + 128], (8, 128))
    for d in range(1, 4):
        pltpu.make_async_remote_copy(
            src_ref=names,
            dst_ref=names_in.at[d - 1],
            send_sem=name_send,
            recv_sem=name_recv,
            device_id=(z * 4 + lax.rem(x + d, 4), ax),
            device_id_type=MESH,
        ).start()
    fr[:, 240:256, :] = jnp.zeros((3, 16, 128), F32)

    along_x(u, a)
    along_yz(u, a)
    lift(a, own_face(u), -LIFT)

    row = nbv_ref[...]
    inside = row < ROWS
    slot = row - ROWS
    device = slot // E
    slot = slot - E * device
    start = BLOCK * device
    upper_row = (~inside) & (slot >= 24)
    where_v[0:6, 0:E] = jnp.where(inside, far + row + 48 * (row // E), start + slot)
    where_v[8:14, 0:E] = jnp.where(
        inside, far + 2 * ROWS + row, start + 96 + slot - jnp.where(upper_row, 24, 0)
    )
    where_copy = pltpu.make_async_copy(where_v, where, where_sem)
    where_copy.start()
    folds = upper_row.astype(F32)
    diagonal = lax.broadcasted_iota(jnp.int32, (E, E), 0) == lax.broadcasted_iota(
        jnp.int32, (E, E), 1
    )
    for f in range(6):
        upper[f * E : f * E + E, :] = jnp.dot(
            jnp.where(diagonal, folds[f : f + 1, :], 0.0),
            jnp.ones((E, 128), F32),
            preferred_element_type=F32,
        )
    where_copy.wait()
    for h in (2, 1, 3, 4):
        gather.hop(h)
    gather.finish()
    facing(0)
    lift(a, from_wt, LIFT)

    publish(a, 1)
    gather2 = Gather(1)
    gather2.start()
    along_x(a, b)
    along_yz(a, b)
    lift(b, own_face(a), -LIFT)
    b[...] = 0.5 * (u[...] + b[...])
    maps = over_lanes(maps_ref[...])
    for h in range(2):
        mt[h] = maps[:, 128 * h : 128 * h + 128]

    def set_place(s, ref):
        label = jnp.concatenate([ref[0, 0:1, :], ref[1, 0:1, :]], axis=1).astype(jnp.int32)
        rows = lax.broadcasted_iota(jnp.int32, (256, 256), 0)
        place[s] = (rows == label).astype(F32).astype(BF16)

    set_place(0, names)
    moved(names_in, name_send, name_recv).wait_recv()
    for d in range(1, 4):
        set_place(d, names_in.at[d - 1])
    gather2.hop(2)
    gather2.hop(1)
    gather2.hop(3)
    gather2.hop(4)
    gather2.finish()
    facing(1)
    lift(b, from_wt, 0.5 * LIFT)

    def coef(h, which, out):
        return lambda k: mt[h, pl.ds(64 * which + 8 * out + k, 1), :]

    @pl.loop(0, 8)
    def _(y):
        for h in range(2):
            rows = [pl.ds(pl.multiple_of(64 * i + 8 * y, 8), 8) for i in range(8)]
            tiles = [b[h, rows[i], :] for i in range(8)]
            for r in range(8):
                b2[h, rows[r], :] = contract(coef(h, 1, r), tiles)

    @pl.loop(0, 8)
    def _(r):
        for h in range(2):
            tiles = [b2[h, pl.ds(64 * r + q, 8, stride=8), :] for q in range(8)]
            for q in range(8):
                a[h, pl.ds(64 * r + q, 8, stride=8), :] = contract(coef(h, 2, q), tiles)

    def sample(tp):
        @pl.loop(0, 8)
        def _(r):
            for h in range(2):
                rows = [pl.ds(pl.multiple_of(64 * r + 8 * i, 8), 8) for i in range(8)]
                tiles = [a[h, rows[i], :] for i in range(8)]
                for t in (2 * tp, 2 * tp + 1):
                    xs[r % 4, h, r // 4, 8 * t : 8 * t + 8, :] = contract(coef(h, 0, t), tiles)

    def piece(ref, tp):
        return ref.at[:, :, pl.ds(16 * tp, 16), :]

    def x_copy(d, tp):
        target = lax.rem(x + d, 4)
        return pltpu.make_async_remote_copy(
            src_ref=piece(xs.at[target], tp),
            dst_ref=piece(xr.at[d - 1], tp),
            send_sem=x_send,
            recv_sem=x_recv.at[tp],
            device_id=(z * 4 + target, ax),
            device_id_type=MESH,
        )

    for tp in range(4):
        sample(tp)
        for d in (2, 1, 3):
            x_copy(d, tp).start()

    wide = lax.broadcasted_iota(jnp.int32, (32, 256), 1)

    def collect(ref, tp, s):
        rows = pl.ds(16 * tp, 16)
        values = jnp.concatenate(
            [ref[0, :, rows, :].reshape(32, 128), ref[1, :, rows, :].reshape(32, 128)], axis=1
        )
        high = values.astype(BF16).astype(F32)
        part = 0.0
        for term in (high, values - high):
            stack = jnp.concatenate(
                [
                    jnp.where((wide >= E * c) & (wide < E * c + E), term, 0.0).astype(BF16)
                    for c in range(C)
                ],
                axis=0,
            )
            part = part + lax.dot_general(
                stack, place[s], (((1,), (1,)), ((), ())), preferred_element_type=F32
            )
        return part

    low8 = lane < 64

    def x_finish(tp):
        part = collect(xs.at[x], tp, 0)
        moved(xr.at[:, :, :, pl.ds(16 * tp, 16), :], x_send, x_recv.at[tp]).wait_recv()
        for d in (1, 3, 2):
            part = part + collect(xr.at[d - 1], tp, d)
        for c in range(C):
            for r2 in range(2):
                o = 32 * c + 16 * r2
                for v in range(2):
                    even = part[o : o + 8, 128 * v : 128 * v + 128]
                    odd = part[o + 8 : o + 16, 128 * v : 128 * v + 128]
                    zs[4 * v + r2, tp, c] = jnp.where(low8, even, pltpu.roll(odd, 64, 1))
                    zs[4 * v + 2 + r2, tp, c] = jnp.where(low8, pltpu.roll(even, 64, 1), odd)

    def z_plan(k, tp):
        long = (tp < 2) == (k == 0)
        if tp in CHAINED:
            return [(r, 1) for r in ((4, 3, 2, 1) if long else (3, 2, 1))]
        return ([(4, 2)] if long else []) + [(3, 1), (2, 2), (1, 1)]

    z_slots = {}
    z_sems = {}
    for tp in range(4):
        for k in range(2):
            for n, (reach, step) in enumerate(z_plan(k, tp)):
                z_slots[k, tp, reach] = n
                if reach > step:
                    z_sems.setdefault((k, tp, reach - step), len(z_sems))

    def z_copy(k, tp, reach):
        step = dict(z_plan(k, tp))[reach]
        way = (1, 7)[k]
        return pltpu.make_async_remote_copy(
            src_ref=zs.at[lax.rem(z + way * reach, 8), tp],
            dst_ref=zr.at[z_slots[k, tp, reach], k, tp],
            send_sem=z_send,
            recv_sem=z_recv.at[z_sems[k, tp, reach - step]] if reach > step else z_last,
            device_id=(lax.rem(z + way * step, 8) * 4 + x, ax),
            device_id_type=MESH,
        )

    def z_send_on(tp, reach):
        for k in range(2):
            plan = dict(z_plan(k, tp))
            if reach not in plan:
                continue
            coming = [z_slots[k, tp, r] for r, step in plan.items() if r - step == reach]
            if coming:
                size = len(coming)
                moved(
                    zr.at[pl.ds(coming[0], size), k, tp], z_send, z_recv.at[z_sems[k, tp, reach]]
                ).wait_recv()
                target = lax.rem(z + (1, 7)[k] * reach, 8)
                more = zr[coming[0], k, tp]
                if size > 1:
                    more = more + zr[coming[1], k, tp]
                zs[target, tp] += more
            z_copy(k, tp, reach).start()

    def z_stage(tp, n):
        if tp in CHAINED:
                rounds = [[4], [3], [2], [1]]
        else:
            rounds = [[4, 3], [2, 1], [], []]
        if 0 <= n < 4:
            for reach in rounds[n]:
                z_send_on(tp, reach)

    for n in range(4):
        for h in range(2):
            flat[128 * h : 128 * h + 128, 128 * n : 128 * n + 128] = b[
                h, 128 * n : 128 * n + 128, :
            ].T
    new_copy = pltpu.make_async_copy(flat.at[0 : C * E], new_ref, new_sem)
    new_copy.start()

    for stage in range(8):
        if stage < 4:
            x_finish(stage)
        for tp in reversed(range(4)):
            z_stage(tp, stage - tp)
    moved(zr.at[pl.ds(0, Z_ENDS // 4), 0], z_send, z_last).wait_recv()
    for tp in range(4):
        total = zs[z, tp]
        for k in range(2):
            for reach, step in z_plan(k, tp):
                if reach == step:
                    total = total + zr[z_slots[k, tp, reach], k, tp]
        sum_ref[tp] = total

    sum_copy = pltpu.make_async_copy(sum_ref, sum_hbm, state_sem.at[0])
    sum_copy.start()
    new_copy.wait()
    gather.drain()
    gather2.drain()
    moved(names_in, name_send, name_recv).wait_send()
    moved(xr, x_send, x_recv.at[0]).wait_send()
    moved(zr.at[pl.ds(0, 3), 0], z_send, z_last).wait_send()
    moved(zr.at[pl.ds(0, 4), 1], z_send, z_last).wait_send()
    sum_copy.wait()


def finish(
    rows_ref,
    sum_hbm,
    table_hbm,
    twiddle_hbm,
    new_ref,
    spec_hbm,
    rows,
    sum_ref,
    table_ref,
    twiddle_ref,
    spec_ref,
    in_sem,
    small_sem,
    out_sem,
):
    def move(k, arriving):
        part = pl.ds(48 * k, 48)
        if arriving:
            return pltpu.make_async_copy(rows_ref.at[part], rows.at[part], in_sem.at[k])
        return pltpu.make_async_copy(rows.at[part], new_ref.at[part], out_sem.at[k])

    small = [
        pltpu.make_async_copy(src, dst, small_sem.at[k])
        for k, (src, dst) in enumerate(
            ((sum_hbm, sum_ref), (table_hbm, table_ref), (twiddle_hbm, twiddle_ref))
        )
    ]
    for copy in small:
        copy.start()
    for k in range(C):
        move(k, True).start()
    for copy in small:
        copy.wait()
    for k in range(C):
        move(k, True).wait()
        move(k, False).start()
    series = sum_ref[...].reshape(4 * C * 8, 128)
    high = series.astype(BF16)
    low = (series - high.astype(F32)).astype(BF16)
    points = (
        jnp.dot(high, table_ref[0], preferred_element_type=F32)
        + jnp.dot(low, table_ref[0], preferred_element_type=F32)
        + jnp.dot(high, table_ref[1], preferred_element_type=F32)
    )
    for v in range(4):
        real, imag = 0.0, 0.0
        for t in range(8):
            span = slice(8 * C * (t // 2), 8 * C * (t // 2) + 8 * C)
            re = points[span, 256 * (t % 2) : 256 * (t % 2) + 128]
            im = points[span, 256 * (t % 2) + 128 : 256 * (t % 2) + 256]
            wr = twiddle_ref[0, t : t + 1, 128 * v : 128 * v + 128]
            wi = twiddle_ref[1, t : t + 1, 128 * v : 128 * v + 128]
            real = real + (re * wr - im * wi)
            imag = imag + (re * wi + im * wr)
        spec_ref[0, :, 128 * v : 128 * v + 128] = real
        spec_ref[1, :, 128 * v : 128 * v + 128] = imag
    spec_copy = pltpu.make_async_copy(spec_ref, spec_hbm, small_sem.at[3])
    spec_copy.start()
    spec_copy.wait()
    for k in range(C):
        move(k, False).wait()


def per_device(n_ax, state, velocity, interp_maps, neighbours, send_faces, owner_device, owner_block):
    vmem = pl.BlockSpec(memory_space=pltpu.VMEM)
    hbm = pl.BlockSpec(memory_space=pl.ANY)
    dma = pltpu.SemaphoreType.DMA
    half_nodes = pltpu.VMEM((2, 512, 128), F32)
    rows, sums = pl.pallas_call(
        functools.partial(kernel, n_ax),
        out_shape=(
            jax.ShapeDtypeStruct((C * E, 512), F32),
            jax.ShapeDtypeStruct((4, C, 8, 128), F32),
        ),
        in_specs=[hbm] * 7,
        out_specs=(hbm, hbm),
        scratch_shapes=[
            pltpu.VMEM((4, C, 8, 128), F32),
            pltpu.VMEM((256, 512), F32),
            half_nodes,
            half_nodes,
            half_nodes,
            half_nodes,
            pltpu.VMEM((3, 2, 8, 128), F32),
            pltpu.VMEM((2, 192, 128), F32),
            pltpu.VMEM((3, 256, 128), F32),
            pltpu.VMEM((3, ROWS, 128), F32),
            pltpu.VMEM((E, 128), F32),
            pltpu.VMEM((BLOCK * n_ax + 3 * ROWS, 128), F32),
            pltpu.VMEM((BLOCK * n_ax + 3 * ROWS, 128), F32),
            pltpu.VMEM((3, ROWS, 128), F32),
            pltpu.VMEM((16, 128), jnp.int32),
            pltpu.SMEM((16, 128), jnp.int32),
            pltpu.VMEM((ROWS, 128), F32),
            pltpu.VMEM((3, E), F32),
            pltpu.VMEM((192, E), F32),
            pltpu.VMEM((1, E), jnp.int32),
            pltpu.VMEM((1, E), jnp.int32),
            pltpu.VMEM((6, E), jnp.int32),
            pltpu.SMEM((1, E), jnp.int32),
            dma((6,)),
            dma,
            pltpu.VMEM((2, 384, 128), F32),
            pltpu.VMEM((2, 8, 128), F32),
            pltpu.VMEM((3, 2, 8, 128), F32),
            pltpu.VMEM((4, 256, 256), BF16),
            pltpu.VMEM((4, 2, 2, 64, 128), F32),
            pltpu.VMEM((3, 2, 2, 64, 128), F32),
            pltpu.VMEM((8, 4, C, 8, 128), F32),
            pltpu.VMEM((4, 2, 4, C, 8, 128), F32),
            dma((2,)),
            dma,
            dma((2,)),
            dma((2, 2, 4, 2)),
            dma((2,)),
            dma,
            dma,
            dma,
            dma((4,)),
            dma,
            dma((Z_STEPS,)),
            dma,
        ],
        compiler_params=pltpu.CompilerParams(
            collective_id=0, has_side_effects=True, vmem_limit_bytes=56 * 1024 * 1024
        ),
        name="advance",
    )(
        velocity.T,
        interp_maps.transpose(1, 2, 3, 0).reshape(192, E),
        owner_device.reshape(1, E),
        owner_block.reshape(1, E),
        neighbours.T,
        send_faces.reshape(1, E),
        state.transpose(1, 0, 2).reshape(C * E, 512),
    )
    new, spec = pl.pallas_call(
        finish,
        out_shape=(
            jax.ShapeDtypeStruct((C * E, 512), F32),
            jax.ShapeDtypeStruct((2, 8 * C, 512), F32),
        ),
        in_specs=[hbm] * 4,
        out_specs=(hbm, hbm),
        scratch_shapes=[
            pltpu.VMEM((C * E, 512), F32),
            pltpu.VMEM((4, C, 8, 128), F32),
            pltpu.VMEM((2, 128, 512), BF16),
            pltpu.VMEM((2, 8, 512), F32),
            pltpu.VMEM((2, 8 * C, 512), F32),
            dma((C,)),
            dma((4,)),
            dma((C,)),
        ],
        name="spectra",
    )(rows, sums, jnp.asarray(TABLES), jnp.asarray(TWIDDLE))
    return (
        new.reshape(C, E, 512).transpose(1, 0, 2),
        spec.reshape(2, C, 8, 512),
    )


def solution(mesh):
    return jax.shard_map(
        functools.partial(per_device, mesh.shape["ax"]),
        mesh=mesh,
        in_specs=(
            P(("az", "ax"), None, None),
            P(("az", "ax"), None),
            P(("az", "ax"), None, None, None),
            P(("az", "ax"), None),
            P(("az", "ax")),
            P(("az", "ax"), None),
            P(("az", "ax")),
        ),
        out_specs=(P(("az", "ax"), None, None), P(None, None, ("az", "ax"), None)),
        check_vma=False,
    )
```

time: 80.2 us -> 61.7 us (0.77)
  the two profiles are of different devices: /device:TPU:8 before, /device:TPU:2 now
where the time goes in v1:
time: 61.7 us; the launch traced here: 61.6 us
  Pallas kernels  60.9 us (99%)
  between operations  0.64 us (1%)
    pallas_call x1, Pallas kernels, per_device(): pl.pallas_call(functools.partial(kernel, n_ax), out_shape=(jax.ShapeDtype...  58.5 us
    pallas_call x1, Pallas kernels, per_device(): pl.pallas_call(finish, out_shape=(jax.ShapeDtypeStruct((C * E, 512), F32)...  2.41 us

profile of v1, /device:TPU:2, one launch (start us, length us, event | category | flops | bytes accessed | tf_op | source)
XLA Modules:
  0.0 61.6 jit_solution(8033555146571418068)
XLA Ops:
  0.6 58.5 %advance.1 = (f32[240,512]{1,0:T(8,128)}, f32[4,5,8,128]{3,2,1,0:T(8,128)}) custom-call(f32[3,48]{1,0:T(4,128)} %bitcast.18, f32[192,48]{1,0:T(8,128)} %bitcast.16, s32[1,48]{1,0:T(1,128)} %bitcast.19, s32[1,48]{1,0:T(1,128)} %bitcast.20, s32[6,48]{1,0:T(8,128)} %bitcast.17, s32[1,48]{1,0:T(1,128)} %bitcast.21, f32[240,512]{1,0:T(8,128)} %bitcast.15), custom_call_target="tpu_custom_call" | custom-call | tf_op jit(solution)/shard_map/advance/pallas_call | solution.py:735
  59.2 2.4 %spectra.1 = (f32[240,512]{1,0:T(8,128)}, f32[2,40,512]{2,1,0:T(8,128)}) custom-call(f32[240,512]{1,0:T(8,128)} %get-tuple-element.6.rows_ref, f32[4,5,8,128]{3,2,1,0:T(8,128)} %get-tuple-element.7.sum_hbm, bf16[2,128,512]{2,1,0:T(8,128)(2,1)} %constant.4.clone.table_hbm, f32[2,8,512]{2,1,0:T(8,128)} %constant.5.clone.twiddle_hbm), custom_call_target="tpu_custom_call" | custom-call | tf_op jit(solution)/shard_map/spectra/pallas_call | solution.py:803

commit v2 on v1

v2 whole, which is shorter than its diff:
```python
import functools

import jax
import jax.numpy as jnp
import ml_dtypes
import numpy as np
from jax import lax
from jax.experimental import pallas as pl
from jax.experimental.pallas import tpu as pltpu
from jax.sharding import PartitionSpec as P

MESH = pl.DeviceIdType.MESH
F32 = jnp.float32
BF16 = jnp.bfloat16
E = 48
C = 5
ROWS = 6 * E
COUNTS = (48, 48, 24)
RISING = (24, 24, 16)
FIELDS = (2, 2, 1)
STEP = 0.02
LIFT = 0.02 * 5.0


def spectral_derivative():
    points = np.cos(np.pi * np.arange(8) / 7.0)
    ends = (np.arange(8) == 0) | (np.arange(8) == 7)
    scales = np.where(ends, 2.0, 1.0)
    signs = np.where(np.arange(8) % 2 == 0, 1.0, -1.0)
    differ = points[:, None] - points[None, :]
    offdiag = (
        scales[:, None]
        / scales[None, :]
        * signs[:, None]
        * signs[None, :]
        / np.where(np.eye(8) > 0, 1.0, differ)
    )
    inner = -points / (2.0 * np.where(ends, 1.0, 1.0 - points * points))
    corner = (2.0 * 49.0 + 1.0) / 6.0
    diagonal = np.where(np.arange(8) == 0, corner, np.where(np.arange(8) == 7, -corner, inner))
    return np.where(np.eye(8) > 0, diagonal[:, None], offdiag)


DERIV = [[float(np.float32(v)) for v in row] for row in spectral_derivative()]


def dft_tables():
    j, m0 = np.meshgrid(np.arange(64), np.arange(64), indexing="ij")
    angle = (j * m0 % 64) * (2.0 * np.pi / 64)
    points = np.concatenate([np.cos(angle)] * 2 + [-np.sin(angle)] * 2, axis=1)
    table = np.zeros((2, 64, 2, 256))
    table[0, :, 0], table[1, :, 1] = points, points
    table = table.reshape(128, 512)
    high = table.astype(ml_dtypes.bfloat16)
    low = (table - high.astype(np.float64)).astype(ml_dtypes.bfloat16)
    t, m = np.meshgrid(np.arange(8), np.arange(512), indexing="ij")
    angle = (t * m % 512) * (2.0 * np.pi / 512)
    twiddle = np.stack([np.cos(angle), -np.sin(angle)]) * 512**-0.5
    return np.stack([high, low]), twiddle.astype(np.float32)


TABLES, TWIDDLE = dft_tables()


def contract(coef, tiles):
    total = coef(0) * tiles[0]
    for k in range(1, len(tiles)):
        total = total + coef(k) * tiles[k]
    return total


def kernel(
    n_ax,
    vel_hbm,
    maps_hbm,
    owner_hbm,
    block_hbm,
    nbv_hbm,
    send_hbm,
    state_ref,
    new_ref,
    sum_hbm,
    sum_ref,
    flat,
    u,
    a,
    b,
    b2,
    vel,
    mt,
    fr,
    local,
    last,
    tab_a0,
    tab_b0,
    tab_c0,
    tab_a1,
    tab_b1,
    tab_c1,
    gat,
    where_v,
    where,
    upper,
    vel_ref,
    maps_ref,
    owner_ref,
    block_ref,
    nbv_ref,
    send_ref,
    wt,
    names,
    names_in,
    place,
    place_c,
    xs,
    xc,
    xr,
    xrc,
    zs,
    zr,
    in_sem,
    where_sem,
    state_sem,
    new_sem,
    ag_send,
    y_recv,
    sib_recv,
    name_send,
    name_recv,
    x_send,
    x_recv,
    z_send,
    z_recv,
    z_last,
):
    az, ax = lax.axis_index("az"), lax.axis_index("ax")
    z, x = az // 4, az % 4
    up, dn = lax.rem(ax + 2, n_ax), lax.rem(ax + n_ax - 2, n_ax)
    up2, dn2 = lax.rem(ax + 4, n_ax), lax.rem(ax + n_ax - 4, n_ax)
    sib = ax + 1 - 2 * lax.rem(ax, 2)
    tabs = ((tab_a0, tab_b0, tab_c0), (tab_a1, tab_b1, tab_c1))

    state_copies = [
        pltpu.make_async_copy(
            state_ref.at[pl.ds(96 * G, E * FIELDS[G])],
            flat.at[G, pl.ds(0, E * FIELDS[G])],
            state_sem.at[G],
        )
        for G in range(3)
    ]
    operand_copies = [
        pltpu.make_async_copy(src, dst, in_sem.at[n])
        for n, (src, dst) in enumerate(
            (
                (send_hbm, send_ref),
                (vel_hbm, vel_ref),
                (owner_hbm, owner_ref),
                (block_hbm, block_ref),
                (nbv_hbm, nbv_ref),
                (maps_hbm, maps_ref),
            )
        )
    ]
    for copy in state_copies + operand_copies:
        copy.start()
    barrier = pltpu.get_barrier_semaphore()
    for peer in (up, dn, up2, dn2, sib):
        pl.semaphore_signal(barrier, inc=1, device_id=(az, peer), device_id_type=MESH)
    for d in range(1, 4):
        pl.semaphore_signal(
            barrier, inc=1, device_id=(z * 4 + lax.rem(x + d, 4), ax), device_id_type=MESH
        )
    for d in (1, 2, 6, 7):
        pl.semaphore_signal(
            barrier, inc=1, device_id=(lax.rem(z + d, 8) * 4 + x, ax), device_id_type=MESH
        )

    def low_half(rows):
        return lax.broadcasted_iota(jnp.int32, (rows, 128), 1) < 64

    def moved(ref, send, recv):
        return pltpu.make_async_remote_copy(
            src_ref=ref,
            dst_ref=ref,
            send_sem=send,
            recv_sem=recv,
            device_id=(az, sib),
            device_id_type=MESH,
        )

    def load(G):
        width = E * FIELDS[G]
        flat[G, width:128] = jnp.zeros((128 - width, 512), F32)
        state_copies[G].wait()
        for n in range(4):
            u[G, 128 * n : 128 * n + 128, :] = flat[G, :, 128 * n : 128 * n + 128].T

    def face_pair(ref, G, pair):
        if pair == 0:
            return jnp.concatenate([ref[G, 0:64, :], ref[G, 448:512, :]], axis=0)
        if pair == 1:
            return jnp.concatenate(
                [ref[G, 64 * i + o : 64 * i + o + 8, :] for o in (0, 56) for i in range(8)], axis=0
            )
        return jnp.concatenate(
            [ref[G, pl.ds(0, 64, stride=8), :], ref[G, pl.ds(7, 64, stride=8), :]], axis=0
        )

    def publish(ref, g, G):
        table = tabs[g][G]
        low = low_half(48)
        for pair in range(3):
            turned = face_pair(ref, G, pair).T
            first = turned[0:48]
            second = turned[48:96]
            even = jnp.where(low, first, pltpu.roll(second, 64, 1))
            odd = jnp.where(low, pltpu.roll(first, 64, 1), second)
            for o, rows in ((0, even), (1, odd)):
                f = 2 * pair + o
                local[G, pl.ds(f, 48, stride=6), :] = rows
                table[pl.ds(f, 48, stride=6), :] = rows
        own = pl.multiple_of(ROWS + COUNTS[G] * ax, 8)

        @pl.loop(0, 6)
        def _(i):
            for k in range(8):
                s = 8 * i + k
                row = local[G, pl.ds(send_ref[0, s], 1), :]
                if G < 2:
                    table[pl.ds(own + s, 1), :] = row
                else:
                    last[pl.ds(s, 1), :] = row

        if G == 2:
            table[pl.ds(own, 24), :] = jnp.where(
                low_half(24), last[0:24, :], pltpu.roll(last[24:48, :], 64, 1)
            )

    def ag_copy(g, source, G, part, target, recv):
        start, count = 0, COUNTS[G]
        if part == 0:
            count = RISING[G]
        if part == 1:
            start, count = RISING[G], COUNTS[G] - RISING[G]
        rows = pl.ds(pl.multiple_of(ROWS + COUNTS[G] * source + start, 8), count)
        return pltpu.make_async_remote_copy(
            src_ref=tabs[g][G].at[rows, :],
            dst_ref=tabs[g][G].at[rows, :],
            send_sem=ag_send.at[g, G],
            recv_sem=recv,
            device_id=(az, target),
            device_id_type=MESH,
        )

    def behind(way, h):
        return lax.rem(ax + (n_ax - 2 * h if way == 0 else 2 * h), n_ax)

    WHOLE = 2
    ways = ((0, up, up2), (1, dn, dn2))

    def share(g, source, G, part):
        ag_copy(g, source, G, part, sib, sib_recv.at[g, G]).start()

    def ag_start(g, G):
        for way, _, two in ways:
            ag_copy(g, ax, G, WHOLE, two, y_recv.at[g, G, way, 1]).start()
        for way, one, _ in ways:
            ag_copy(g, ax, G, WHOLE, one, y_recv.at[g, G, way, 0]).start()
        share(g, ax, G, WHOLE)

    def ag_take(g, G, h):
        for way, one, two in ways:
            source = behind(way, h)
            part = WHOLE if h < 4 else way
            ag_copy(g, source, G, part, one, y_recv.at[g, G, way, h - 1]).wait_recv()
            if h == 2:
                ag_copy(g, source, G, way, two, y_recv.at[g, G, way, 3]).start()
                ag_copy(g, source, G, WHOLE, one, y_recv.at[g, G, way, 2]).start()
            share(g, source, G, part)

    def ag_rest(g, G):
        for h in (1, 3, 4):
            ag_take(g, G, h)
        moved(
            tabs[g][G].at[pl.ds(0, 8 * COUNTS[G]), :], ag_send.at[g, G], sib_recv.at[g, G]
        ).wait_recv()

    def along_x(src, dst, G):
        @pl.loop(0, 8)
        def _(y):
            rows = [pl.ds(pl.multiple_of(64 * i + 8 * y, 8), 8) for i in range(8)]
            tiles = [src[G, rows[i], :] for i in range(8)]
            v = vel[0]
            for i in range(8):
                dst[G, rows[i], :] = tiles[i] + v * contract(lambda k: DERIV[i][k], tiles)

    def along_yz(src, dst, G):
        @pl.loop(0, 8)
        def _(i):
            rows = [pl.ds(pl.multiple_of(64 * i + 8 * y, 8), 8) for y in range(8)]
            tiles = [src[G, rows[y], :] for y in range(8)]
            v = vel[1]
            for y in range(8):
                dst[G, rows[y], :] += v * contract(lambda k: DERIV[y][k], tiles)
            cols = [pl.ds(64 * i + q, 8, stride=8) for q in range(8)]
            tiles = [src[G, cols[q], :] for q in range(8)]
            v = vel[2]
            for q in range(8):
                dst[G, cols[q], :] += v * contract(lambda k: DERIV[q][k], tiles)

    def lift(dst, G, value, scale):
        dst[G, 0:64, :] += scale * value(0)
        dst[G, 448:512, :] += scale * value(1)
        for f, o in ((2, 0), (3, 56)):
            rows = scale * value(f)
            for i in range(8):
                dst[G, 64 * i + o : 64 * i + o + 8, :] += rows[8 * i : 8 * i + 8]
        dst[G, pl.ds(0, 64, stride=8), :] += scale * value(4)
        dst[G, pl.ds(7, 64, stride=8), :] += scale * value(5)

    def advance(src, dst, G):
        along_x(src, dst, G)
        along_yz(src, dst, G)

        def own_face(f):
            return face_pair(src, G, f // 2)[64 * (f % 2) : 64 * (f % 2) + 64]

        lift(dst, G, own_face, -LIFT)

    def facing(g, G, dst, scale):
        table = tabs[g][G]

        @pl.loop(0, E // 2)
        def _(i):
            for k in range(2):
                e = 2 * i + k
                for f in range(6):
                    row = where[8 * (G // 2) + f, e]
                    gat[pl.ds(f * E + e, 1), :] = table[pl.ds(row, 1), :]

        def got(f):
            rows = gat[f * E : f * E + E, :]
            if G < 2:
                return rows
            return jnp.where(upper[f * E : f * E + E, :] > 0.5, pltpu.roll(rows, 64, 1), rows)

        low = low_half(48)
        for pair in range(3):
            first, second = got(2 * pair), got(2 * pair + 1)
            fr[pair, 0:48, :] = jnp.where(low, first, pltpu.roll(second, 64, 1))
            fr[pair, 48:96, :] = (
                jnp.where(low, pltpu.roll(first, 64, 1), second)
                if G < 2
                else jnp.zeros((48, 128), F32)
            )
            wt[128 * pair : 128 * pair + 128, :] = fr[pair].T
        lift(dst, G, lambda f: wt[64 * f : 64 * f + 64, :], scale)

    fr[:, 96:128, :] = jnp.zeros((3, 32, 128), F32)
    for G in range(3):
        load(G)
        if G == 0:
            operand_copies[0].wait()
        publish(u, 0, G)
        if G == 0:
            pl.semaphore_wait(barrier, 12)
        ag_start(0, G)
    for copy in operand_copies[1:]:
        copy.wait()

    lane = lax.broadcasted_iota(jnp.int32, (E, 128), 1)
    element = lax.broadcasted_iota(jnp.int32, (E, 128), 0)
    spread = ((lane == element) | (lane == element + E)).astype(F32)

    def over_lanes(rows):
        return jnp.dot(rows, spread, precision=lax.Precision.HIGHEST, preferred_element_type=F32)

    speeds = over_lanes(-STEP * vel_ref[...])
    block = block_ref[...]
    label = lax.rem(block, 4) * 64 + owner_ref[...] * 2 + block // 4
    names[...] = jnp.broadcast_to(over_lanes(label.astype(F32)), (8, 128))
    for d in range(3):
        vel[d] = jnp.broadcast_to(speeds[d : d + 1], (8, 128))
    for d in range(1, 4):
        pltpu.make_async_remote_copy(
            src_ref=names,
            dst_ref=names_in.at[d - 1],
            send_sem=name_send,
            recv_sem=name_recv,
            device_id=(z * 4 + lax.rem(x + d, 4), ax),
            device_id_type=MESH,
        ).start()

    row = nbv_ref[...]
    slot = row - ROWS
    device = slot // E
    slot = slot - E * device
    upper_row = (row >= ROWS) & (slot >= 24)
    where_v[0:6, 0:E] = row
    where_v[8:14, 0:E] = jnp.where(
        row < ROWS, row, ROWS + 24 * device + slot - jnp.where(upper_row, 24, 0)
    )
    where_copy = pltpu.make_async_copy(where_v, where, where_sem)
    where_copy.start()
    folds = upper_row.astype(F32)
    diagonal = lax.broadcasted_iota(jnp.int32, (E, E), 0) == lax.broadcasted_iota(
        jnp.int32, (E, E), 1
    )
    for f in range(6):
        upper[f * E : f * E + E, :] = jnp.dot(
            jnp.where(diagonal, folds[f : f + 1, :], 0.0),
            jnp.ones((E, 128), F32),
            preferred_element_type=F32,
        )

    def coef(which, out):
        return lambda k: mt[pl.ds(64 * which + 8 * out + k, 1), :]

    def sample(G):
        @pl.loop(0, 8)
        def _(y):
            rows = [pl.ds(pl.multiple_of(64 * i + 8 * y, 8), 8) for i in range(8)]
            tiles = [b[G, rows[i], :] for i in range(8)]
            for r in range(8):
                b2[rows[r], :] = contract(coef(1, r), tiles)

        @pl.loop(0, 8)
        def _(r):
            cols = [pl.ds(64 * r + q, 8, stride=8) for q in range(8)]
            tiles = [b2[cols[q], :] for q in range(8)]
            for q in range(8):
                a[G, cols[q], :] = contract(coef(2, q), tiles)

        @pl.loop(0, 4)
        def _(r):
            low = low_half(8)
            for t in range(8):
                both = []
                for r2 in range(2):
                    tiles = [
                        a[G, pl.ds(pl.multiple_of(64 * (r + 4 * r2) + 8 * i, 8), 8), :]
                        for i in range(8)
                    ]
                    both.append(contract(coef(0, t), tiles))
                if G < 2:
                    for r2 in range(2):
                        xs[r, G, r2, 8 * t : 8 * t + 8, :] = both[r2]
                else:
                    xc[r, 8 * t : 8 * t + 8, :] = jnp.where(
                        low, both[0], pltpu.roll(both[1], 64, 1)
                    )

    def x_send_all(G):
        for d in (2, 1, 3):
            target = lax.rem(x + d, 4)
            pltpu.make_async_remote_copy(
                src_ref=xs.at[target, G] if G < 2 else xc.at[target],
                dst_ref=xr.at[G, d - 1] if G < 2 else xrc.at[d - 1],
                send_sem=x_send,
                recv_sem=x_recv.at[G],
                device_id=(z * 4 + target, ax),
                device_id_type=MESH,
            ).start()

    def set_places():
        moved(names_in, name_send, name_recv).wait_recv()
        rows = lax.broadcasted_iota(jnp.int32, (256, 128), 0)
        lanes = lax.broadcasted_iota(jnp.int32, (1, 128), 1)
        for s in range(4):
            name = (names[0:1, :] if s == 0 else names_in[s - 1, 0:1, :]).astype(jnp.int32)
            place[:, 128 * s : 128 * s + 128] = (rows == name).astype(F32).astype(BF16)
            name = jnp.where(
                lanes < 64, name, pltpu.roll(names[0:1, :] if s == 0 else names_in[s - 1, 0:1, :], 64, 1).astype(jnp.int32)
            )
            place_c[:, 128 * s : 128 * s + 128] = (rows == name).astype(F32).astype(BF16)

    low8 = low_half(8)

    def x_finish(G):
        if G < 2:
            moved(xr.at[G], x_send, x_recv.at[G]).wait_recv()
            sources = [xs[x, G]] + [xr[G, d] for d in range(3)]
            values = jnp.concatenate([v.reshape(128, 128) for v in sources], axis=1)
            width = E
        else:
            moved(xrc, x_send, x_recv.at[G]).wait_recv()
            values = jnp.concatenate([xc[x]] + [xrc[d] for d in range(3)], axis=1)
            width = 64
        names_of = place if G < 2 else place_c
        wide = lax.rem(lax.broadcasted_iota(jnp.int32, values.shape, 1), 128)
        high = values.astype(BF16).astype(F32)
        part = 0.0
        for term in (high, values - high):
            stack = jnp.concatenate(
                [
                    jnp.where((wide >= width * k) & (wide < width * k + E), term, 0.0).astype(BF16)
                    for k in range(2)
                ],
                axis=0,
            )
            part = part + lax.dot_general(
                stack, names_of[...], (((1,), (1,)), ((), ())), preferred_element_type=F32
            )
        for c in range(FIELDS[G]):
            for r2 in range(2):
                for tp in range(4):
                    o = 128 * c + 64 * r2 + 16 * tp
                    for v in range(2):
                        even = part[o : o + 8, 128 * v : 128 * v + 128]
                        odd = part[o + 8 : o + 16, 128 * v : 128 * v + 128]
                        zs[4 * v + r2, G, tp // 2, c, tp % 2] = jnp.where(
                            low8, even, pltpu.roll(odd, 64, 1)
                        )
                        zs[4 * v + 2 + r2, G, tp // 2, c, tp % 2] = jnp.where(
                            low8, pltpu.roll(even, 64, 1), odd
                        )

    def z_copy(kind, k, G, half):
        reach, step = ((4, 2), (3, 1), (2, 2), (1, 1))[kind]
        way = (1, 7)[k]
        fields = pl.ds(0, FIELDS[G])
        return pltpu.make_async_remote_copy(
            src_ref=zs.at[lax.rem(z + way * reach, 8), G, half, fields],
            dst_ref=zr.at[G, half, k, kind, fields],
            send_sem=z_send,
            recv_sem=z_recv.at[G, half, k] if kind < 2 else z_last.at[G, half],
            device_id=(lax.rem(z + way * step, 8) * 4 + x, ax),
            device_id_type=MESH,
        )

    def z_first(G):
        for half in range(2):
            z_copy(0, half, G, half).start()
            for k in range(2):
                z_copy(1, k, G, half).start()

    def z_second(G):
        fields = pl.ds(0, FIELDS[G])
        for half in range(2):
            for k in (1 - half, half):
                target = lax.rem(z + (2, 6)[k], 8)
                least = 0 if k == half else 1
                moved(
                    zr.at[G, half, k, pl.ds(least, 2 - least), fields],
                    z_send,
                    z_recv.at[G, half, k],
                ).wait_recv()
                more = zr[G, half, k, 1, fields]
                if k == half:
                    more = more + zr[G, half, k, 0, fields]
                zs[target, G, half, fields] += more
                z_copy(2, k, G, half).start()
        for half in range(2):
            for k in range(2):
                z_copy(3, k, G, half).start()

    def new_rows(G):
        for n in range(4):
            flat[G, :, 128 * n : 128 * n + 128] = b[G, 128 * n : 128 * n + 128, :].T
        copy = pltpu.make_async_copy(
            flat.at[G, pl.ds(0, E * FIELDS[G])],
            new_ref.at[pl.ds(96 * G, E * FIELDS[G])],
            new_sem.at[G],
        )
        copy.start()
        return copy

    def first_section(G):
        facing(0, G, a, LIFT)
        publish(a, 1, G)
        ag_start(1, G)

    def second_base(G):
        advance(a, b, G)
        b[G] = 0.5 * (u[G] + b[G])

    def second_section(G):
        facing(1, G, b, 0.5 * LIFT)

    for G in range(3):
        advance(u, a, G)
    where_copy.wait()
    for G in range(3):
        ag_take(0, G, 2)
    ag_rest(0, 0)
    first_section(0)
    ag_rest(0, 1)
    first_section(1)
    ag_rest(0, 2)
    first_section(2)
    ag_take(1, 0, 2)
    second_base(0)
    mt[...] = over_lanes(maps_ref[...])
    ag_take(1, 1, 2)
    second_base(1)
    ag_take(1, 2, 2)
    second_base(2)
    set_places()
    for G in range(3):
        ag_rest(1, G)
        second_section(G)
        sample(G)
        x_send_all(G)
        if G == 2:
            x_finish(0)
            z_first(0)
    x_finish(1)
    z_first(1)
    new_copies = [new_rows(G) for G in range(3)]
    z_second(0)
    x_finish(2)
    z_first(2)
    z_second(1)
    z_second(2)
    for G in range(3):
        for half in range(2):
            moved(
                zr.at[G, half, :, pl.ds(2, 2), pl.ds(0, FIELDS[G])], z_send, z_last.at[G, half]
            ).wait_recv()
    for G in range(3):
        for half in range(2):
            for c in range(FIELDS[G]):
                total = zs[z, G, half, c]
                for kind in (3, 2):
                    for k in range(2):
                        total = total + zr[G, half, k, kind, c]
                for tp in range(2):
                    sum_ref[2 * half + tp, 2 * G + c] = total[tp]

    sum_copy = pltpu.make_async_copy(sum_ref, sum_hbm, in_sem.at[0])
    sum_copy.start()
    for copy in new_copies:
        copy.wait()
    for g in range(2):
        for G in range(3):
            moved(
                tabs[g][G].at[pl.ds(0, 15 * COUNTS[G]), :], ag_send.at[g, G], sib_recv.at[g, G]
            ).wait_send()
    moved(names_in, name_send, name_recv).wait_send()
    for G in range(2):
        moved(xr.at[G], x_send, x_recv.at[0]).wait_send()
    moved(xrc, x_send, x_recv.at[0]).wait_send()
    for G in range(3):
        for half in range(2):
            fields = pl.ds(0, FIELDS[G])
            moved(
                zr.at[G, half, :, pl.ds(1, 3), fields], z_send, z_last.at[0, 0]
            ).wait_send()
            moved(zr.at[G, half, 0, 0, fields], z_send, z_last.at[0, 0]).wait_send()
    sum_copy.wait()


def finish(
    rows_ref,
    sum_hbm,
    table_hbm,
    twiddle_hbm,
    new_ref,
    spec_hbm,
    rows,
    sum_ref,
    table_ref,
    twiddle_ref,
    spec_ref,
    in_sem,
    small_sem,
    out_sem,
):
    def move(k, arriving):
        part = pl.ds(48 * k, 48)
        if arriving:
            return pltpu.make_async_copy(rows_ref.at[part], rows.at[part], in_sem.at[k])
        return pltpu.make_async_copy(rows.at[part], new_ref.at[part], out_sem.at[k])

    small = [
        pltpu.make_async_copy(src, dst, small_sem.at[k])
        for k, (src, dst) in enumerate(
            ((sum_hbm, sum_ref), (table_hbm, table_ref), (twiddle_hbm, twiddle_ref))
        )
    ]
    for copy in small:
        copy.start()
    for k in range(C):
        move(k, True).start()
    for copy in small:
        copy.wait()
    for k in range(C):
        move(k, True).wait()
        move(k, False).start()
    series = sum_ref[...].reshape(4 * C * 8, 128)
    high = series.astype(BF16)
    low = (series - high.astype(F32)).astype(BF16)
    points = (
        jnp.dot(high, table_ref[0], preferred_element_type=F32)
        + jnp.dot(low, table_ref[0], preferred_element_type=F32)
        + jnp.dot(high, table_ref[1], preferred_element_type=F32)
    )
    for v in range(4):
        real, imag = 0.0, 0.0
        for t in range(8):
            span = slice(8 * C * (t // 2), 8 * C * (t // 2) + 8 * C)
            re = points[span, 256 * (t % 2) : 256 * (t % 2) + 128]
            im = points[span, 256 * (t % 2) + 128 : 256 * (t % 2) + 256]
            wr = twiddle_ref[0, t : t + 1, 128 * v : 128 * v + 128]
            wi = twiddle_ref[1, t : t + 1, 128 * v : 128 * v + 128]
            real = real + (re * wr - im * wi)
            imag = imag + (re * wi + im * wr)
        spec_ref[0, :, 128 * v : 128 * v + 128] = real
        spec_ref[1, :, 128 * v : 128 * v + 128] = imag
    spec_copy = pltpu.make_async_copy(spec_ref, spec_hbm, small_sem.at[3])
    spec_copy.start()
    spec_copy.wait()
    for k in range(C):
        move(k, False).wait()


def per_device(n_ax, state, velocity, interp_maps, neighbours, send_faces, owner_device, owner_block):
    vmem = pl.BlockSpec(memory_space=pltpu.VMEM)
    hbm = pl.BlockSpec(memory_space=pl.ANY)
    dma = pltpu.SemaphoreType.DMA
    nodes = pltpu.VMEM((3, 512, 128), F32)
    rows, sums = pl.pallas_call(
        functools.partial(kernel, n_ax),
        out_shape=(
            jax.ShapeDtypeStruct((C * E, 512), F32),
            jax.ShapeDtypeStruct((4, C, 8, 128), F32),
        ),
        in_specs=[hbm] * 7,
        out_specs=(hbm, hbm),
        scratch_shapes=[
            pltpu.VMEM((4, C, 8, 128), F32),
            pltpu.VMEM((3, 128, 512), F32),
            nodes,
            nodes,
            nodes,
            pltpu.VMEM((512, 128), F32),
            pltpu.VMEM((3, 8, 128), F32),
            pltpu.VMEM((192, 128), F32),
            pltpu.VMEM((3, 128, 128), F32),
            pltpu.VMEM((3, ROWS, 128), F32),
            pltpu.VMEM((E, 128), F32),
            *[pltpu.VMEM((ROWS + n * n_ax, 128), F32) for n in COUNTS * 2],
            pltpu.VMEM((ROWS, 128), F32),
            pltpu.VMEM((16, 128), jnp.int32),
            pltpu.SMEM((16, 128), jnp.int32),
            pltpu.VMEM((ROWS, 128), F32),
            pltpu.VMEM((3, E), F32),
            pltpu.VMEM((192, E), F32),
            pltpu.VMEM((1, E), jnp.int32),
            pltpu.VMEM((1, E), jnp.int32),
            pltpu.VMEM((6, E), jnp.int32),
            pltpu.SMEM((1, E), jnp.int32),
            pltpu.VMEM((384, 128), F32),
            pltpu.VMEM((8, 128), F32),
            pltpu.VMEM((3, 8, 128), F32),
            pltpu.VMEM((256, 512), BF16),
            pltpu.VMEM((256, 512), BF16),
            pltpu.VMEM((4, 2, 2, 64, 128), F32),
            pltpu.VMEM((4, 64, 128), F32),
            pltpu.VMEM((2, 3, 2, 64, 128), F32),
            pltpu.VMEM((3, 64, 128), F32),
            pltpu.VMEM((8, 3, 2, 2, 2, 8, 128), F32),
            pltpu.VMEM((3, 2, 2, 4, 2, 2, 8, 128), F32),
            dma((6,)),
            dma,
            dma((3,)),
            dma((3,)),
            dma((2, 3)),
            dma((2, 3, 2, 4)),
            dma((2, 3)),
            dma,
            dma,
            dma,
            dma((3,)),
            dma,
            dma((3, 2, 2)),
            dma((3, 2)),
        ],
        compiler_params=pltpu.CompilerParams(
            collective_id=0, has_side_effects=True, vmem_limit_bytes=56 * 1024 * 1024
        ),
        name="advance",
    )(
        velocity.T,
        interp_maps.transpose(1, 2, 3, 0).reshape(192, E),
        owner_device.reshape(1, E),
        owner_block.reshape(1, E),
        neighbours.T,
        send_faces.reshape(1, E),
        state.transpose(1, 0, 2).reshape(C * E, 512),
    )
    new, spec = pl.pallas_call(
        finish,
        out_shape=(
            jax.ShapeDtypeStruct((C * E, 512), F32),
            jax.ShapeDtypeStruct((2, 8 * C, 512), F32),
        ),
        in_specs=[hbm] * 4,
        out_specs=(hbm, hbm),
        scratch_shapes=[
            pltpu.VMEM((C * E, 512), F32),
            pltpu.VMEM((4, C, 8, 128), F32),
            pltpu.VMEM((2, 128, 512), BF16),
            pltpu.VMEM((2, 8, 512), F32),
            pltpu.VMEM((2, 8 * C, 512), F32),
            dma((C,)),
            dma((4,)),
            dma((C,)),
        ],
        name="spectra",
    )(rows, sums, jnp.asarray(TABLES), jnp.asarray(TWIDDLE))
    return (
        new.reshape(C, E, 512).transpose(1, 0, 2),
        spec.reshape(2, C, 8, 512),
    )


def solution(mesh):
    return jax.shard_map(
        functools.partial(per_device, mesh.shape["ax"]),
        mesh=mesh,
        in_specs=(
            P(("az", "ax"), None, None),
            P(("az", "ax"), None),
            P(("az", "ax"), None, None, None),
            P(("az", "ax"), None),
            P(("az", "ax")),
            P(("az", "ax"), None),
            P(("az", "ax")),
        ),
        out_specs=(P(("az", "ax"), None, None), P(None, None, ("az", "ax"), None)),
        check_vma=False,
    )
```

time: 61.7 us -> 58.7 us (0.951)
  the two profiles are of different devices: /device:TPU:2 before, /device:TPU:8 now
where the time goes in v2:
time: 58.7 us; the launch traced here: 58.5 us
  Pallas kernels  57.9 us (99%)
  between operations  0.64 us (1%)
    pallas_call x1, Pallas kernels, per_device(): pl.pallas_call(functools.partial(kernel, n_ax), out_shape=(jax.ShapeDtype...  55.5 us
    pallas_call x1, Pallas kernels, per_device(): pl.pallas_call(finish, out_shape=(jax.ShapeDtypeStruct((C * E, 512), F32)...  2.41 us

profile of v2, /device:TPU:8, one launch (start us, length us, event | category | flops | bytes accessed | tf_op | source)
XLA Modules:
  0.0 58.5 jit_solution(7408340959501562577)
XLA Ops:
  0.6 55.5 %advance.1 = (f32[240,512]{1,0:T(8,128)}, f32[4,5,8,128]{3,2,1,0:T(8,128)}) custom-call(f32[3,48]{1,0:T(4,128)} %bitcast.18, f32[192,48]{1,0:T(8,128)} %bitcast.16, s32[1,48]{1,0:T(1,128)} %bitcast.19, s32[1,48]{1,0:T(1,128)} %bitcast.20, s32[6,48]{1,0:T(8,128)} %bitcast.17, s32[1,48]{1,0:T(1,128)} %bitcast.21, f32[240,512]{1,0:T(8,128)} %bitcast.15), custom_call_target="tpu_custom_call" | custom-call | tf_op jit(solution)/shard_map/advance/pallas_call | solution.py:722
  56.1 2.4 %spectra.1 = (f32[240,512]{1,0:T(8,128)}, f32[2,40,512]{2,1,0:T(8,128)}) custom-call(f32[240,512]{1,0:T(8,128)} %get-tuple-element.6.rows_ref, f32[4,5,8,128]{3,2,1,0:T(8,128)} %get-tuple-element.7.sum_hbm, bf16[2,128,512]{2,1,0:T(8,128)(2,1)} %constant.4.clone.table_hbm, f32[2,8,512]{2,1,0:T(8,128)} %constant.5.clone.twiddle_hbm), custom_call_target="tpu_custom_call" | custom-call | tf_op jit(solution)/shard_map/spectra/pallas_call | solution.py:792

commit v3 on v2

--- a/solution.py
+++ b/solution.py
@@ -18,6 +18,7 @@
 COUNTS = (48, 48, 24)
 RISING = (24, 24, 16)
 FIELDS = (2, 2, 1)
+ORDER = (2, 0, 1)
 STEP = 0.02
 LIFT = 0.02 * 5.0
 
@@ -78,9 +79,12 @@
     nbv_hbm,
     send_hbm,
     state_ref,
+    table_hbm,
+    twiddle_hbm,
     new_ref,
-    sum_hbm,
     sum_ref,
+    table_ref,
+    twiddle_ref,
     flat,
     u,
     a,
@@ -121,7 +125,6 @@
     in_sem,
     where_sem,
     state_sem,
-    new_sem,
     ag_send,
     y_recv,
     sib_recv,
@@ -158,6 +161,8 @@
                 (block_hbm, block_ref),
                 (nbv_hbm, nbv_ref),
                 (maps_hbm, maps_ref),
+                (table_hbm, table_ref),
+                (twiddle_hbm, twiddle_ref),
             )
         )
     ]
@@ -356,16 +361,17 @@
             wt[128 * pair : 128 * pair + 128, :] = fr[pair].T
         lift(dst, G, lambda f: wt[64 * f : 64 * f + 64, :], scale)
 
+    one, two, three = ORDER
     fr[:, 96:128, :] = jnp.zeros((3, 32, 128), F32)
-    for G in range(3):
+    operand_copies[0].wait()
+    for G in ORDER:
         load(G)
-        if G == 0:
-            operand_copies[0].wait()
         publish(u, 0, G)
-        if G == 0:
+        if G == one:
             pl.semaphore_wait(barrier, 12)
-        ag_start(0, G)
-    for copy in operand_copies[1:]:
+        if G != three:
+            ag_start(0, G)
+    for copy in operand_copies[1:6]:
         copy.wait()
 
     lane = lax.broadcasted_iota(jnp.int32, (E, 128), 1)
@@ -431,17 +437,16 @@
             for q in range(8):
                 a[G, cols[q], :] = contract(coef(2, q), tiles)
 
+    def sample_half(G, half):
         @pl.loop(0, 4)
         def _(r):
             low = low_half(8)
-            for t in range(8):
-                both = []
-                for r2 in range(2):
-                    tiles = [
-                        a[G, pl.ds(pl.multiple_of(64 * (r + 4 * r2) + 8 * i, 8), 8), :]
-                        for i in range(8)
-                    ]
-                    both.append(contract(coef(0, t), tiles))
+            tiles = [
+                [a[G, pl.ds(pl.multiple_of(64 * (r + 4 * r2) + 8 * i, 8), 8), :] for i in range(8)]
+                for r2 in range(2)
+            ]
+            for t in range(4 * half, 4 * half + 4):
+                both = [contract(coef(0, t), tiles[r2]) for r2 in range(2)]
                 if G < 2:
                     for r2 in range(2):
                         xs[r, G, r2, 8 * t : 8 * t + 8, :] = both[r2]
@@ -450,14 +455,24 @@
                         low, both[0], pltpu.roll(both[1], 64, 1)
                     )
 
-    def x_send_all(G):
+    def x_half(ref, G, half):
+        rows = pl.ds(32 * half, 32)
+        return ref.at[:, rows, :] if G < 2 else ref.at[rows, :]
+
+    def x_from(G, d):
+        return xr.at[G, d] if G < 2 else xrc.at[d]
+
+    def x_to(G, d):
+        return xs.at[d, G] if G < 2 else xc.at[d]
+
+    def x_start(G, half):
         for d in (2, 1, 3):
             target = lax.rem(x + d, 4)
             pltpu.make_async_remote_copy(
-                src_ref=xs.at[target, G] if G < 2 else xc.at[target],
-                dst_ref=xr.at[G, d - 1] if G < 2 else xrc.at[d - 1],
+                src_ref=x_half(x_to(G, target), G, half),
+                dst_ref=x_half(x_from(G, d - 1), G, half),
                 send_sem=x_send,
-                recv_sem=x_recv.at[G],
+                recv_sem=x_recv.at[G, half],
                 device_id=(z * 4 + target, ax),
                 device_id_type=MESH,
             ).start()
@@ -476,16 +491,13 @@
 
     low8 = low_half(8)
 
-    def x_finish(G):
-        if G < 2:
-            moved(xr.at[G], x_send, x_recv.at[G]).wait_recv()
-            sources = [xs[x, G]] + [xr[G, d] for d in range(3)]
-            values = jnp.concatenate([v.reshape(128, 128) for v in sources], axis=1)
-            width = E
-        else:
-            moved(xrc, x_send, x_recv.at[G]).wait_recv()
-            values = jnp.concatenate([xc[x]] + [xrc[d] for d in range(3)], axis=1)
-            width = 64
+    def x_finish(G, half):
+        rows = pl.ds(32 * half, 32)
+        arrived = xr.at[G, :, :, rows] if G < 2 else xrc.at[:, rows]
+        moved(arrived, x_send, x_recv.at[G, half]).wait_recv()
+        sources = [x_half(x_to(G, x), G, half)] + [x_half(x_from(G, d), G, half) for d in range(3)]
+        values = jnp.concatenate([v[...].reshape(-1, 128) for v in sources], axis=1)
+        width = E if G < 2 else 64
         names_of = place if G < 2 else place_c
         wide = lax.rem(lax.broadcasted_iota(jnp.int32, values.shape, 1), 128)
         high = values.astype(BF16).astype(F32)
@@ -503,17 +515,18 @@
             )
         for c in range(FIELDS[G]):
             for r2 in range(2):
-                for tp in range(4):
-                    o = 128 * c + 64 * r2 + 16 * tp
+                for tp in range(2):
+                    o = 64 * c + 32 * r2 + 16 * tp
                     for v in range(2):
                         even = part[o : o + 8, 128 * v : 128 * v + 128]
                         odd = part[o + 8 : o + 16, 128 * v : 128 * v + 128]
-                        zs[4 * v + r2, G, tp // 2, c, tp % 2] = jnp.where(
+                        zs[4 * v + r2, G, half, c, tp] = jnp.where(
                             low8, even, pltpu.roll(odd, 64, 1)
                         )
-                        zs[4 * v + 2 + r2, G, tp // 2, c, tp % 2] = jnp.where(
+                        zs[4 * v + 2 + r2, G, half, c, tp] = jnp.where(
                             low8, pltpu.roll(even, 64, 1), odd
                         )
+        z_first(G, half)
 
     def z_copy(kind, k, G, half):
         reach, step = ((4, 2), (3, 1), (2, 2), (1, 1))[kind]
@@ -528,42 +541,32 @@
             device_id_type=MESH,
         )
 
-    def z_first(G):
-        for half in range(2):
-            z_copy(0, half, G, half).start()
-            for k in range(2):
-                z_copy(1, k, G, half).start()
-
-    def z_second(G):
+    def z_first(G, half):
+        z_copy(0, half, G, half).start()
+        for k in (half, 1 - half):
+            z_copy(1, k, G, half).start()
+
+    def z_second(G, half):
         fields = pl.ds(0, FIELDS[G])
-        for half in range(2):
-            for k in (1 - half, half):
-                target = lax.rem(z + (2, 6)[k], 8)
-                least = 0 if k == half else 1
-                moved(
-                    zr.at[G, half, k, pl.ds(least, 2 - least), fields],
-                    z_send,
-                    z_recv.at[G, half, k],
-                ).wait_recv()
-                more = zr[G, half, k, 1, fields]
-                if k == half:
-                    more = more + zr[G, half, k, 0, fields]
-                zs[target, G, half, fields] += more
-                z_copy(2, k, G, half).start()
-        for half in range(2):
-            for k in range(2):
-                z_copy(3, k, G, half).start()
+        for k in (1 - half, half):
+            target = lax.rem(z + (2, 6)[k], 8)
+            least = 0 if k == half else 1
+            moved(
+                zr.at[G, half, k, pl.ds(least, 2 - least), fields], z_send, z_recv.at[G, half, k]
+            ).wait_recv()
+            more = zr[G, half, k, 1, fields]
+            if k == half:
+                more = more + zr[G, half, k, 0, fields]
+            zs[target, G, half, fields] += more
+            z_copy(2, k, G, half).start()
+        for k in range(2):
+            z_copy(3, k, G, half).start()
 
     def new_rows(G):
+        width = E * FIELDS[G]
         for n in range(4):
-            flat[G, :, 128 * n : 128 * n + 128] = b[G, 128 * n : 128 * n + 128, :].T
-        copy = pltpu.make_async_copy(
-            flat.at[G, pl.ds(0, E * FIELDS[G])],
-            new_ref.at[pl.ds(96 * G, E * FIELDS[G])],
-            new_sem.at[G],
-        )
-        copy.start()
-        return copy
+            turned = b[G, 128 * n : 128 * n + 128, :].T
+            new_ref[96 * G : 96 * G + width, 128 * n : 128 * n + 128] = turned[0:width]
 
     def first_section(G):
         facing(0, G, a, LIFT)
@@ -576,42 +579,53 @@
 
     def second_section(G):
         facing(1, G, b, 0.5 * LIFT)
-
+        sample(G)
+        for half in range(2):
+            sample_half(G, half)
+            x_start(G, half)
+
+    advance(u, a, one)
+    advance(u, a, two)
+    ag_take(0, one, 2)
+    ag_start(0, three)
+    advance(u, a, three)
+    where_copy.wait()
+    ag_take(0, two, 2)
+    ag_rest(0, one)
+    first_section(one)
+    ag_take(0, three, 2)
+    ag_rest(0, two)
+    first_section(two)
+    mt[...] = over_lanes(maps_ref[...])
+    second_base(one)
+    ag_take(1, one, 2)
+    ag_rest(0, three)
+    first_section(three)
+    second_base(two)
+    ag_take(1, two, 2)
+    set_places()
+    ag_rest(1, one)
+    second_section(one)
+    second_base(three)
+    ag_take(1, three, 2)
+    ag_rest(1, two)
+    second_section(two)
+    x_finish(one, 0)
+    x_finish(one, 1)
+    ag_rest(1, three)
+    second_section(three)
+    z_second(one, 0)
+    z_second(one, 1)
+    x_finish(two, 0)
+    x_finish(two, 1)
     for G in range(3):
-        advance(u, a, G)
-    where_copy.wait()
-    for G in range(3):
-        ag_take(0, G, 2)
-    ag_rest(0, 0)
-    first_section(0)
-    ag_rest(0, 1)
-    first_section(1)
-    ag_rest(0, 2)
-    first_section(2)
-    ag_take(1, 0, 2)
-    second_base(0)
-    mt[...] = over_lanes(maps_ref[...])
-    ag_take(1, 1, 2)
-    second_base(1)
-    ag_take(1, 2, 2)
-    second_base(2)
-    set_places()
-    for G in range(3):
-        ag_rest(1, G)
-        second_section(G)
-        sample(G)
-        x_send_all(G)
-        if G == 2:
-            x_finish(0)
-            z_first(0)
-    x_finish(1)
-    z_first(1)
-    new_copies = [new_rows(G) for G in range(3)]
-    z_second(0)
-    x_finish(2)
-    z_first(2)
-    z_second(1)
-    z_second(2)
+        new_rows(G)
+    x_finish(three, 0)
+    z_second(two, 0)
+    x_finish(three, 1)
+    z_second(two, 1)
+    z_second(three, 0)
+    z_second(three, 1)
     for G in range(3):
         for half in range(2):
             moved(
@@ -627,9 +641,7 @@
                 for tp in range(2):
                     sum_ref[2 * half + tp, 2 * G + c] = total[tp]
 
-    sum_copy = pltpu.make_async_copy(sum_ref, sum_hbm, in_sem.at[0])
-    sum_copy.start()
-    for copy in new_copies:
+    for copy in operand_copies[6:]:
         copy.wait()
     for g in range(2):
         for G in range(3):
@@ -638,8 +650,8 @@
             ).wait_send()
     moved(names_in, name_send, name_recv).wait_send()
     for G in range(2):
-        moved(xr.at[G], x_send, x_recv.at[0]).wait_send()
-    moved(xrc, x_send, x_recv.at[0]).wait_send()
+        moved(xr.at[G], x_send, x_recv.at[0, 0]).wait_send()
+    moved(xrc, x_send, x_recv.at[0, 0]).wait_send()
     for G in range(3):
         for half in range(2):
             fields = pl.ds(0, FIELDS[G])
@@ -647,46 +659,13 @@
                 zr.at[G, half, :, pl.ds(1, 3), fields], z_send, z_last.at[0, 0]
             ).wait_send()
             moved(zr.at[G, half, 0, 0, fields], z_send, z_last.at[0, 0]).wait_send()
-    sum_copy.wait()
 
 
 def finish(
-    rows_ref,
-    sum_hbm,
-    table_hbm,
-    twiddle_hbm,
-    new_ref,
-    spec_hbm,
-    rows,
-    sum_ref,
-    table_ref,
-    twiddle_ref,
-    spec_ref,
-    in_sem,
-    small_sem,
-    out_sem,
+    rows_ref, sum_ref, table_ref, twiddle_ref, new_ref, spec_hbm, spec_ref, out_sem
 ):
-    def move(k, arriving):
-        part = pl.ds(48 * k, 48)
-        if arriving:
-            return pltpu.make_async_copy(rows_ref.at[part], rows.at[part], in_sem.at[k])
-        return pltpu.make_async_copy(rows.at[part], new_ref.at[part], out_sem.at[k])
-
-    small = [
-        pltpu.make_async_copy(src, dst, small_sem.at[k])
-        for k, (src, dst) in enumerate(
-            ((sum_hbm, sum_ref), (table_hbm, table_ref), (twiddle_hbm, twiddle_ref))
-        )
-    ]
-    for copy in small:
-        copy.start()
-    for k in range(C):
-        move(k, True).start()
-    for copy in small:
-        copy.wait()
-    for k in range(C):
-        move(k, True).wait()
-        move(k, False).start()
+    new_copy = pltpu.make_async_copy(rows_ref, new_ref, out_sem.at[0])
+    new_copy.start()
     series = sum_ref[...].reshape(4 * C * 8, 128)
     high = series.astype(BF16)
     low = (series - high.astype(F32)).astype(BF16)
@@ -707,11 +686,10 @@
             imag = imag + (re * wi + im * wr)
         spec_ref[0, :, 128 * v : 128 * v + 128] = real
         spec_ref[1, :, 128 * v : 128 * v + 128] = imag
-    spec_copy = pltpu.make_async_copy(spec_ref, spec_hbm, small_sem.at[3])
+    spec_copy = pltpu.make_async_copy(spec_ref, spec_hbm, out_sem.at[1])
     spec_copy.start()
     spec_copy.wait()
-    for k in range(C):
-        move(k, False).wait()
+    new_copy.wait()
 
 
 def per_device(n_ax, state, velocity, interp_maps, neighbours, send_faces, owner_device, owner_block):
@@ -719,16 +697,17 @@
     hbm = pl.BlockSpec(memory_space=pl.ANY)
     dma = pltpu.SemaphoreType.DMA
     nodes = pltpu.VMEM((3, 512, 128), F32)
-    rows, sums = pl.pallas_call(
+    handed = pl.pallas_call(
         functools.partial(kernel, n_ax),
         out_shape=(
-            jax.ShapeDtypeStruct((C * E, 512), F32),
-            jax.ShapeDtypeStruct((4, C, 8, 128), F32),
+            pltpu.VMEM((C * E, 512), F32),
+            pltpu.VMEM((4, C, 8, 128), F32),
+            pltpu.VMEM(TABLES.shape, BF16),
+            pltpu.VMEM(TWIDDLE.shape, F32),
         ),
-        in_specs=[hbm] * 7,
-        out_specs=(hbm, hbm),
+        in_specs=[hbm] * 9,
+        out_specs=(vmem,) * 4,
         scratch_shapes=[
-            pltpu.VMEM((4, C, 8, 128), F32),
             pltpu.VMEM((3, 128, 512), F32),
             nodes,
             nodes,
@@ -761,9 +740,8 @@
             pltpu.VMEM((3, 64, 128), F32),
             pltpu.VMEM((8, 3, 2, 2, 2, 8, 128), F32),
             pltpu.VMEM((3, 2, 2, 4, 2, 2, 8, 128), F32),
-            dma((6,)),
+            dma((8,)),
             dma,
-            dma((3,)),
             dma((3,)),
             dma((2, 3)),
             dma((2, 3, 2, 4)),
@@ -771,7 +749,7 @@
             dma,
             dma,
             dma,
-            dma((3,)),
+            dma((3, 2)),
             dma,
             dma((3, 2, 2)),
             dma((3, 2)),
@@ -788,6 +766,8 @@
         neighbours.T,
         send_faces.reshape(1, E),
         state.transpose(1, 0, 2).reshape(C * E, 512),
+        jnp.asarray(TABLES),
+        jnp.asarray(TWIDDLE),
     )
     new, spec = pl.pallas_call(
         finish,
@@ -795,20 +775,11 @@
             jax.ShapeDtypeStruct((C * E, 512), F32),
             jax.ShapeDtypeStruct((2, 8 * C, 512), F32),
         ),
-        in_specs=[hbm] * 4,
+        in_specs=[vmem] * 4,
         out_specs=(hbm, hbm),
-        scratch_shapes=[
-            pltpu.VMEM((C * E, 512), F32),
-            pltpu.VMEM((4, C, 8, 128), F32),
-            pltpu.VMEM((2, 128, 512), BF16),
-            pltpu.VMEM((2, 8, 512), F32),
-            pltpu.VMEM((2, 8 * C, 512), F32),
-            dma((C,)),
-            dma((4,)),
-            dma((C,)),
-        ],
+        scratch_shapes=[pltpu.VMEM((2, 8 * C, 512), F32), dma((2,))],
         name="spectra",
-    )(rows, sums, jnp.asarray(TABLES), jnp.asarray(TWIDDLE))
+    )(*[pltpu.with_memory_space_constraint(array, pltpu.VMEM) for array in handed])
     return (
         new.reshape(C, E, 512).transpose(1, 0, 2),
         spec.reshape(2, C, 8, 512),

time: 58.7 us -> 55.9 us (0.952)
  Pallas kernels: 57.9 us -> 55.1 us
    pallas_call x1, Pallas kernels: 55.5 us -> 54 us  [per_device(): pl.pallas_call(functools.partial(kernel, n_ax), out_shape=(pltpu.VMEM((C...]
    pallas_call x1, Pallas kernels: 2.41 us -> 1.09 us  [per_device(): pl.pallas_call(finish, out_shape=(jax.ShapeDtypeStruct((C * E, 512), F32)...]
where the time goes in v3:
time: 55.9 us; the launch traced here: 55.8 us
  Pallas kernels  55.1 us (99%)
  between operations  0.64 us (1%)
    pallas_call x1, Pallas kernels, per_device(): pl.pallas_call(functools.partial(kernel, n_ax), out_shape=(pltpu.VMEM((C...  54 us

profile of v3, /device:TPU:8, one launch (start us, length us, event | category | flops | bytes accessed | tf_op | source)
XLA Modules:
  0.0 55.8 jit_solution(20678674967394687)
XLA Ops:
  0.6 54.0 %advance.1 = (f32[240,512]{1,0:T(8,128)S(1)}, f32[4,5,8,128]{3,2,1,0:T(8,128)S(1)}, bf16[2,128,512]{2,1,0:T(8,128)(2,1)S(1)}, f32[2,8,512]{2,1,0:T(8,128)S(1)}) custom-call(f32[3,48]{1,0:T(4,128)} %bitcast.18, f32[192,48]{1,0:T(8,128)} %bitcast.16, s32[1,48]{1,0:T(1,128)} %bitcast.19, s32[1,48]{1,0:T(1,128)} %bitcast.20, s32[6,48]{1,0:T(8,128)} %bitcast.17, ...), custom_call_target="tpu_custom_call" | custom-call | tf_op jit(solution)/shard_map/advance/pallas_call | solution.py:700
  54.7 1.1 %spectra.1 = (f32[240,512]{1,0:T(8,128)}, f32[2,40,512]{2,1,0:T(8,128)}) custom-call(f32[240,512]{1,0:T(8,128)S(1)} %get-tuple-element.8.rows_ref, f32[4,5,8,128]{3,2,1,0:T(8,128)S(1)} %get-tuple-element.9.sum_ref, bf16[2,128,512]{2,1,0:T(8,128)(2,1)S(1)} %get-tuple-element.10.table_ref, f32[2,8,512]{2,1,0:T(8,128)S(1)} %get-tuple-element.11.twiddle_ref), custom_call_target="tpu_custom_call" | custom-call | tf_op jit(solution)/shard_map/spectra/pallas_call | solution.py:772

commit v4 on v3

--- a/solution.py
+++ b/solution.py
@@ -269,9 +269,11 @@
     def ag_start(g, G):
         for way, _, two in ways:
             ag_copy(g, ax, G, WHOLE, two, y_recv.at[g, G, way, 1]).start()
+        share(g, ax, G, WHOLE)
+
+    def ag_near(g, G):
         for way, one, _ in ways:
             ag_copy(g, ax, G, WHOLE, one, y_recv.at[g, G, way, 0]).start()
-        share(g, ax, G, WHOLE)
 
     def ag_take(g, G, h):
         for way, one, two in ways:
@@ -371,6 +373,8 @@
             pl.semaphore_wait(barrier, 12)
         if G != three:
             ag_start(0, G)
+        if G == one:
+            ag_near(0, one)
     for copy in operand_copies[1:6]:
         copy.wait()
 
@@ -543,8 +547,9 @@
 
     def z_first(G, half):
         z_copy(0, half, G, half).start()
-        for k in (half, 1 - half):
-            z_copy(1, k, G, half).start()
+        for kind in (1, 3):
+            for k in (half, 1 - half):
+                z_copy(kind, k, G, half).start()
 
     def z_second(G, half):
         fields = pl.ds(0, FIELDS[G])
@@ -559,8 +564,6 @@
                 more = more + zr[G, half, k, 0, fields]
             zs[target, G, half, fields] += more
             z_copy(2, k, G, half).start()
-        for k in range(2):
-            z_copy(3, k, G, half).start()
 
     def new_rows(G):
         width = E * FIELDS[G]
@@ -591,18 +594,23 @@
     advance(u, a, three)
     where_copy.wait()
     ag_take(0, two, 2)
+    ag_near(0, two)
+    ag_near(0, three)
     ag_rest(0, one)
     first_section(one)
     ag_take(0, three, 2)
+    ag_near(1, one)
     ag_rest(0, two)
     first_section(two)
     mt[...] = over_lanes(maps_ref[...])
     second_base(one)
     ag_take(1, one, 2)
+    ag_near(1, two)
     ag_rest(0, three)
     first_section(three)
     second_base(two)
     ag_take(1, two, 2)
+    ag_near(1, three)
     set_places()
     ag_rest(1, one)
     second_section(one)

time: 55.9 us -> 54.5 us (0.975)
  the two profiles are of different devices: /device:TPU:8 before, /device:TPU:64 now
where the time goes in v4:
time: 54.5 us; the launch traced here: 54.4 us
  Pallas kernels  53.7 us (99%)
  between operations  0.64 us (1%)
    pallas_call x1, Pallas kernels, per_device(): pl.pallas_call(functools.partial(kernel, n_ax), out_shape=(pltpu.VMEM((C...  52.6 us
    pallas_call x1, Pallas kernels, per_device(): pl.pallas_call(finish, out_shape=(jax.ShapeDtypeStruct((C * E, 512), F32)...  1.09 us

profile of v4, /device:TPU:64, one launch (start us, length us, event | category | flops | bytes accessed | tf_op | source)
XLA Modules:
  0.0 54.4 jit_solution(14430735940118947561)
XLA Ops:
  0.6 52.6 %advance.1 = (f32[240,512]{1,0:T(8,128)S(1)}, f32[4,5,8,128]{3,2,1,0:T(8,128)S(1)}, bf16[2,128,512]{2,1,0:T(8,128)(2,1)S(1)}, f32[2,8,512]{2,1,0:T(8,128)S(1)}) custom-call(f32[3,48]{1,0:T(4,128)} %bitcast.18, f32[192,48]{1,0:T(8,128)} %bitcast.16, s32[1,48]{1,0:T(1,128)} %bitcast.19, s32[1,48]{1,0:T(1,128)} %bitcast.20, s32[6,48]{1,0:T(8,128)} %bitcast.17, ...), custom_call_target="tpu_custom_call" | custom-call | tf_op jit(solution)/shard_map/advance/pallas_call | solution.py:708
  53.3 1.1 %spectra.1 = (f32[240,512]{1,0:T(8,128)}, f32[2,40,512]{2,1,0:T(8,128)}) custom-call(f32[240,512]{1,0:T(8,128)S(1)} %get-tuple-element.8.rows_ref, f32[4,5,8,128]{3,2,1,0:T(8,128)S(1)} %get-tuple-element.9.sum_ref, bf16[2,128,512]{2,1,0:T(8,128)(2,1)S(1)} %get-tuple-element.10.table_ref, f32[2,8,512]{2,1,0:T(8,128)S(1)} %get-tuple-element.11.twiddle_ref), custom_call_target="tpu_custom_call" | custom-call | tf_op jit(solution)/shard_map/spectra/pallas_call | solution.py:780

commit v5 on v4

--- a/solution.py
+++ b/solution.py
@@ -614,8 +614,8 @@
     set_places()
     ag_rest(1, one)
     second_section(one)
+    ag_take(1, three, 2)
     second_base(three)
-    ag_take(1, three, 2)
     ag_rest(1, two)
     second_section(two)
     x_finish(one, 0)

time: 54.5 us -> 54.6 us (level)
  the two profiles are of different devices: /device:TPU:64 before, /device:TPU:16 now
where the time goes in v5:
time: 54.6 us; the launch traced here: 54.5 us
  Pallas kernels  53.9 us (99%)
  between operations  0.64 us (1%)
    pallas_call x1, Pallas kernels, per_device(): pl.pallas_call(functools.partial(kernel, n_ax), out_shape=(pltpu.VMEM((C...  52.8 us
    pallas_call x1, Pallas kernels, per_device(): pl.pallas_call(finish, out_shape=(jax.ShapeDtypeStruct((C * E, 512), F32)...  1.1 us

profile of v5, /device:TPU:16, one launch (start us, length us, event | category | flops | bytes accessed | tf_op | source)
XLA Modules:
  0.0 54.5 jit_solution(12478300085060747460)
XLA Ops:
  0.6 52.8 %advance.1 = (f32[240,512]{1,0:T(8,128)S(1)}, f32[4,5,8,128]{3,2,1,0:T(8,128)S(1)}, bf16[2,128,512]{2,1,0:T(8,128)(2,1)S(1)}, f32[2,8,512]{2,1,0:T(8,128)S(1)}) custom-call(f32[3,48]{1,0:T(4,128)} %bitcast.18, f32[192,48]{1,0:T(8,128)} %bitcast.16, s32[1,48]{1,0:T(1,128)} %bitcast.19, s32[1,48]{1,0:T(1,128)} %bitcast.20, s32[6,48]{1,0:T(8,128)} %bitcast.17, ...), custom_call_target="tpu_custom_call" | custom-call | tf_op jit(solution)/shard_map/advance/pallas_call | solution.py:708
  53.4 1.1 %spectra.1 = (f32[240,512]{1,0:T(8,128)}, f32[2,40,512]{2,1,0:T(8,128)}) custom-call(f32[240,512]{1,0:T(8,128)S(1)} %get-tuple-element.8.rows_ref, f32[4,5,8,128]{3,2,1,0:T(8,128)S(1)} %get-tuple-element.9.sum_ref, bf16[2,128,512]{2,1,0:T(8,128)(2,1)S(1)} %get-tuple-element.10.table_ref, f32[2,8,512]{2,1,0:T(8,128)S(1)} %get-tuple-element.11.twiddle_ref), custom_call_target="tpu_custom_call" | custom-call | tf_op jit(solution)/shard_map/spectra/pallas_call | solution.py:780
